TPU v7x, 256 devices: a whole 4x4x8 slice. The times are simulated.
256 devices in a mesh: blk: 64 (over y, x_hi, z), repl: 4 (over x_lo, core).
Axes of the slice: x: 4 (x_hi: 2, x_lo: 2; x = x_hi * 2 + x_lo), y: 4, z: 8, core: 2. Of those that a mesh axis runs over, the one named last changes fastest.
Arguments:
- feats: bfloat16 [131072, 512], P(('blk', 'repl')), may hold values from -6 to 6
- weight: bfloat16 [512, 512], replicated, may hold values from -0.25 to 0.25
- tile_vals: bfloat16 [1024, 8, 128, 128], P(('blk', 'repl')), may hold values from -0.25 to 0.25
- tile_cols: int32 [1024, 8], P(('blk', 'repl')), may hold values from 0 to 1023, as said below
- tile_count: int32 [1024], P(('blk', 'repl')), may hold values from 2 to 8, as said below
- cotangent: bfloat16 [131072, 512], P(('blk', 'repl')), may hold values from -24 to 24
Outputs:
- output: bfloat16 [131072, 512], P(('blk', 'repl'))
- weight_grad: float32 [512, 512], replicated
- feat_grad: bfloat16 [131072, 512], P(('blk', 'repl'))
Inputs may be any that keep to these rules, and one draw needn't show every extreme that they name: `tile_cols`: slot 0 of block row k names k itself. Every named column block lies in a panel (of 2048 nodes, block row k being in panel k * 128 // 2048) at most 2 panels away from its row's panel, counted around a closed cycle of panels. `tile_count`: slots at and after a block row's count are not part of the adjacency.
All inputs are finite; a program needn't handle non-finite values.
Results may differ from a plain program's by a relative error of at most 0.011.
Values may be sent and summed in bfloat16 or wider, within the bound.
A program may use at most 128 MiB of HBM per device.

v0:
```python
import math

import jax
import jax.numpy as jnp
from jax import lax
from jax.sharding import PartitionSpec as P

TILE = 128
SLOTS = 8
REACH = 2


def passed_along(value, axis, steps):
    count = lax.axis_size(axis)
    pairs = [(source, (source + steps) % count) for source in range(count)]
    return lax.ppermute(value, axis, pairs)


def shortened(x):
    return jax.tree.map(lambda a: a.astype(jnp.bfloat16) if a.dtype == jnp.float32 else a, x)


def from_everyone(x, axis):
    length = lax.axis_size(axis)
    return lax.all_to_all(jnp.broadcast_to(x[None], (length, *x.shape)), axis, 0, 0, tiled=True)


def laid_out(pieces, dim):
    lengths = list(pieces.shape[1:])
    lengths[dim] *= pieces.shape[0]
    return jnp.moveaxis(pieces, 0, dim).reshape(lengths)


def gathered_copies(x, axis, dim):
    pieces = from_everyone(x, axis)
    return laid_out(pieces, dim)


def silu_slope(preact):
    sigma = jax.nn.sigmoid(preact)
    return sigma * (1.0 + preact * (1.0 - sigma))


def window_index(tile_cols, center, panel_blocks, cycle_size):
    panel_of = tile_cols // panel_blocks
    offset = (panel_of - center) % cycle_size
    offset = jnp.where(offset > REACH, offset - cycle_size, offset)
    return (offset + REACH) * panel_blocks + tile_cols % panel_blocks


def shift_window(source):
    lower_side = []
    upper_side = []
    below_piece = source
    above_piece = source
    for hop_number in range(REACH):
        below_piece = passed_along(below_piece, "blk", 1)
        above_piece = passed_along(above_piece, "blk", -1)
        lower_side.append(below_piece)
        upper_side.append(above_piece)
    pieces = lower_side[::-1] + [source] + upper_side
    return pieces


def return_to_owners(shares):
    upward = jnp.zeros_like(shares[REACH])
    for offset in range(REACH, 0, -1):
        upward = passed_along(shortened(upward + shares[offset + REACH]), "blk", 1)
    downward = jnp.zeros_like(shares[REACH])
    for offset in range(-REACH, 0):
        downward = passed_along(shortened(downward + shares[offset + REACH]), "blk", -1)
    total = shares[REACH] + upward + downward
    return total


def local(feats, weight, tile_vals, tile_cols, tile_count, cotangent):
    node_rows = feats.shape[0]
    feat_width = feats.shape[1]
    cycle_size = lax.axis_size("blk")
    group_size = lax.axis_size("repl")
    panel_size = node_rows * group_size
    panel_blocks = panel_size // TILE
    block_rows = node_rows // TILE
    span_count = 2 * REACH + 1
    center = lax.axis_index("blk")
    own_panel = gathered_copies(feats, "repl", 0)
    pieces = shift_window(own_panel)
    window = jnp.concatenate(pieces, axis=0).reshape(span_count * panel_blocks, TILE, feat_width)
    local_index = window_index(tile_cols, center, panel_blocks, cycle_size)
    slot_ids = jnp.arange(SLOTS, dtype=jnp.int32)
    live_slots = slot_ids[None, :] < tile_count[:, None]
    masked_vals = jnp.where(live_slots[:, :, None, None], tile_vals, jnp.zeros_like(tile_vals))
    picked = window[local_index]
    summed = jnp.einsum("nsij,nsjf->nif", masked_vals, picked, preferred_element_type=jnp.float32)
    aggregate = summed.reshape(node_rows, feat_width).astype(jnp.bfloat16)
    preact = jnp.dot(aggregate, weight, preferred_element_type=jnp.float32)
    output = jax.nn.silu(preact).astype(jnp.bfloat16)
    slope = (cotangent.astype(jnp.float32) * silu_slope(preact)).astype(jnp.bfloat16)
    nodes_total = node_rows * group_size * cycle_size
    weight_term = jnp.einsum("nf,ng->fg", aggregate, slope, preferred_element_type=jnp.float32)
    weight_grad = lax.psum(weight_term, ("blk", "repl")) * (1.0 / math.sqrt(nodes_total))
    backward = jnp.einsum("nf,gf->ng", slope, weight, preferred_element_type=jnp.float32).astype(
        jnp.bfloat16
    )
    back_blocks = backward.reshape(block_rows, TILE, feat_width)
    segments = span_count * panel_blocks
    contrib = jnp.einsum(
        "nsji,njf->nsif", masked_vals, back_blocks, preferred_element_type=jnp.float32
    )
    partial_sums = jax.ops.segment_sum(
        contrib.reshape(block_rows * SLOTS, TILE, feat_width),
        local_index.reshape(-1),
        num_segments=segments,
    )
    panel_parts = partial_sums.reshape(span_count, panel_size, feat_width)
    shares = [panel_parts[position] for position in range(span_count)]
    panel_total = return_to_owners(shares)
    grad_rows = lax.psum_scatter(
        panel_total.astype(jnp.bfloat16), "repl", scatter_dimension=0, tiled=True
    )
    return (output, weight_grad, grad_rows)


def solution(mesh):
    in_specs = (
        P(("blk", "repl"), None),
        P(),
        P(("blk", "repl"), None, None, None),
        P(("blk", "repl"), None),
        P(("blk", "repl")),
        P(("blk", "repl"), None),
    )
    out_specs = (P(("blk", "repl"), None), P(), P(("blk", "repl"), None))
    return jax.shard_map(local, mesh=mesh, in_specs=in_specs, out_specs=out_specs, check_vma=False)
```

profile of v0, /device:TPU:1, one launch (start us, length us, event | category | flops | bytes accessed | tf_op | source)
XLA Modules:
  0.0 550.8 jit_solution(13088517721672567636)
XLA Ops:
  8.0 0.0 copy-start
  8.0 0.0 copy-start.6
  8.0 0.0 copy-start.8
  8.0 0.0 all-reduce.2.cloned.1.call-start
  8.1 1.2 broadcast_in_dim.28
  9.3 30.3 %all_to_all.5 = bf16[4,512,512]{2,1,0:T(8,128)(2,1)S(1)} all-to-all(bf16[4,512,512]{2,1,0:T(8,128)(2,1)S(1)} %broadcast_in_dim.28), channel_id=1, replica_groups=mesh['blk'=64,'repl'=4] {'repl'}, dimensions={0} | all-to-all | bytes 4194304 | tf_op jit(solution)/shard_map/all_to_all | solution.py:25
  39.6 0.0 collective-permute-start
  39.7 8.8 %collective-permute-start.2 = (bf16[2048,512]{1,0:T(8,128)(2,1)S(1)}, bf16[2048,512]{1,0:T(8,128)(2,1)}, u32[]{:S(2)}, u32[]{:S(2)}) collective-permute-start(bf16[2048,512]{1,0:T(8,128)(2,1)S(1)} %bitcast.42), channel_id=1, source_target_pairs={{0,252},{4,0},{8,4},{12,8},{16,12},{20,16},{24,20},{28,24},{32,28}... | collective-permute-start | bytes 6291464 | tf_op jit(solution)/shard_map/ppermute | solution.py:16
  48.4 45.1 %collective-permute-done = bf16[2048,512]{1,0:T(8,128)(2,1)} collective-permute-done((bf16[2048,512]{1,0:T(8,128)(2,1)S(1)}, bf16[2048,512]{1,0:T(8,128)(2,1)}, u32[]{:S(2)}, u32[]{:S(2)}) %collective-permute-start) | collective-permute-done | bytes 2097184 | tf_op jit(solution)/shard_map/ppermute | solution.py:16
  93.5 0.0 collective-permute-start.1
  93.5 0.0 collective-permute-done.2
  93.5 7.2 %collective-permute-start.3 = (bf16[2048,512]{1,0:T(8,128)(2,1)}, bf16[2048,512]{1,0:T(8,128)(2,1)}, u32[]{:S(2)}, u32[]{:S(2)}) collective-permute-start(bf16[2048,512]{1,0:T(8,128)(2,1)} %collective-permute-done.2), channel_id=1, source_target_pairs={{0,252},{4,0},{8,4},{12,8},{16,12},{20,16},{24,20},{28,24},{32,28}... | collective-permute-start | bytes 6291464 | tf_op jit(solution)/shard_map/ppermute | solution.py:16
  100.7 0.0 copy-done.6
  100.7 0.1 reshape.61
  100.8 0.1 reshape.69
  100.9 0.0 copy-done.8
  100.9 0.1 iota_compare_fusion
  101.0 44.1 %collective-permute-done.1 = bf16[2048,512]{1,0:T(8,128)(2,1)} collective-permute-done((bf16[2048,512]{1,0:T(8,128)(2,1)}, bf16[2048,512]{1,0:T(8,128)(2,1)}, u32[]{:S(2)}, u32[]{:S(2)}) %collective-permute-start.1) | collective-permute-done | bytes 2097184 | tf_op jit(solution)/shard_map/ppermute | solution.py:16
  145.1 1.7 constant_dynamic-update-slice_fusion.4
  146.8 1.7 constant_dynamic-update-slice_fusion.3
  148.6 0.1 constant_dynamic-update-slice_fusion.2
  148.7 1.7 constant_dynamic-update-slice_fusion.1
  150.4 0.0 collective-permute-done.3
  150.4 1.7 constant_dynamic-update-slice_fusion
  152.2 0.0 copy-start.3
  152.2 4.0 copy-done.3
  156.2 7.0 %gather_fusion = bf16[32,128,512]{2,1,0:T(8,128)(2,1)} fusion(bf16[80,128,512]{2,1,0:T(8,128)(2,1)} %bitcast.44, s32[1024]{0:T(1024)S(1)} %pad_clamp_fusion), kind=kCustom, calls=%fused_computation | custom fusion | bytes 8388736 | tf_op jit(solution)/shard_map/gather | solution.py:93
  163.1 0.0 copy-start.7
  163.1 0.0 copy-done.2
  163.1 3.0 fusion.4
  166.2 0.0 copy-start.4
  166.2 0.0 copy-done
  166.2 0.0 copy-done.7
  166.2 1.6 multiply_convert_fusion
  167.8 0.5 convolution_convert_fusion
  168.2 0.0 copy-done.4
  168.2 4.6 fusion.5
  172.9 9.7 %broadcast_in_dim.30 = f32[80,128,512]{2,1,0:T(8,128)} broadcast(f32[]{:T(128)} %constant.63.clone.1), dimensions={} | broadcast | bytes 20971524 | tf_op jit(solution)/shard_map/broadcast_in_dim | solution.py:110
  182.5 18.8 %scatter_fusion = f32[80,128,512]{2,1,0:T(8,128)} fusion(f32[80,128,512]{2,1,0:T(8,128)} %broadcast_in_dim.30, s32[32]{0:T(128)S(1)} %reshape.69, f32[32,128,512]{2,1,0:T(8,128)} %bitcast.39), kind=kCustom, calls=%fused_computation.1 | custom fusion | flops 2097152 | bytes 25165952 | tf_op jit(solution)/shard_map/scatter-add | solution.py:110
  201.4 8.0 %convert.4 = bf16[80,128,512]{2,1,0:T(8,128)(2,1)S(1)} convert(f32[80,128,512]{2,1,0:T(8,128)} %scatter_fusion) | non-fusion elementwise | flops 5242880 | bytes 31457280 | tf_op jit(solution)/shard_map/convert.1
  209.3 2.3 fusion.18
  211.6 1.4 collective-permute-start.6
  213.0 0.1 collective-permute-start.4
  213.1 10.1 %fusion.17 = (f32[16,128,512]{2,1,0:T(8,128)S(1)}, f32[16,128,512]{2,1,0:T(8,128)}, f32[16,128,512]{2,1,0:T(8,128)}) fusion(f32[80,128,512]{2,1,0:T(8,128)} %scatter_fusion), kind=kLoop, calls=%fused_computation.46 | loop fusion | bytes 25165824 | tf_op jit(solution)/shard_map/slice | solution.py:116
  223.2 33.4 %collective-permute-done.6 = bf16[2048,512]{1,0:T(8,128)(2,1)} collective-permute-done((bf16[2048,512]{1,0:T(8,128)(2,1)}, bf16[2048,512]{1,0:T(8,128)(2,1)}, u32[]{:S(2)}, u32[]{:S(2)}) %collective-permute-start.6) | collective-permute-done | bytes 2097184 | tf_op jit(solution)/shard_map/ppermute | solution.py:16
  256.6 4.9 fusion
  261.5 6.6 %collective-permute-start.7 = (bf16[2048,512]{1,0:T(8,128)(2,1)}, bf16[2048,512]{1,0:T(8,128)(2,1)}, u32[]{:S(2)}, u32[]{:S(2)}) collective-permute-start(bf16[2048,512]{1,0:T(8,128)(2,1)} %fusion), channel_id=1, source_target_pairs={{0,252},{4,0},{8,4},{12,8},{16,12},{20,16},{24,20},{28,24},{32,28}... | collective-permute-start | bytes 6291464 | tf_op jit(solution)/shard_map/ppermute | solution.py:16
  268.0 0.0 collective-permute-done.4
  268.1 0.0 copy-start.5
  268.1 4.1 fusion.1
  272.1 0.0 collective-permute-start.5
  272.1 0.0 copy-done.5
  272.1 1.4 fusion.19
  273.6 0.0 all-reduce.2.cloned.1.call-update
  273.6 0.0 reduce-scatter.2.cloned.1.call-start
  273.6 36.6 %collective-permute-done.7 = bf16[2048,512]{1,0:T(8,128)(2,1)} collective-permute-done((bf16[2048,512]{1,0:T(8,128)(2,1)}, bf16[2048,512]{1,0:T(8,128)(2,1)}, u32[]{:S(2)}, u32[]{:S(2)}) %collective-permute-start.7) | collective-permute-done | bytes 2097184 | tf_op jit(solution)/shard_map/ppermute | solution.py:16
  310.2 12.0 %collective-permute-done.5 = bf16[2048,512]{1,0:T(8,128)(2,1)S(1)} collective-permute-done((bf16[2048,512]{1,0:T(8,128)(2,1)}, bf16[2048,512]{1,0:T(8,128)(2,1)S(1)}, u32[]{:S(2)}, u32[]{:S(2)}) %collective-permute-start.5) | collective-permute-done | bytes 2097184 | tf_op jit(solution)/shard_map/ppermute | solution.py:16
  322.3 0.0 copy-start.1
  322.3 5.2 fusion.3
  327.4 0.0 reduce-scatter.2.cloned.1.call-update
  327.4 213.6 %all-reduce.2.cloned.1.call-done = f32[512,512]{1,0:T(8,128)} async-done(((f32[512,512]{1,0:T(8,128)}), f32[512,512]{1,0:T(8,128)}) %all-reduce.2.cloned.1.call-update) | async-done | bytes 1048592 | tf_op jit(solution)/shard_map/psum | solution.py:101
  541.1 2.3 broadcast_multiply_fusion
  543.4 0.0 reduce-scatter.2.cloned.1.call-done
  543.4 0.0 copy-done.1
  (3 shorter events, 0.0 us)
Async XLA Ops:
  8.0 158.2 %copy-start = (bf16[512,512]{1,0:T(8,128)(2,1)S(1)}, bf16[512,512]{1,0:T(8,128)(2,1)}, u32[]{:S(2)}) copy-start(bf16[512,512]{1,0:T(8,128)(2,1)} %param.7) | copy-start | bytes 1572868
  8.0 92.7 %copy-start.6 = (s32[4,8]{1,0:T(4,128)S(1)}, s32[4,8]{1,0:T(4,128)}, u32[]{:S(2)}) copy-start(s32[4,8]{1,0:T(4,128)} %param.9) | copy-start | bytes 388
  8.0 92.9 %copy-start.8 = (s32[4]{0:T(128)S(1)}, s32[4]{0:T(128)}, u32[]{:S(2)}) copy-start(s32[4]{0:T(128)} %param.10) | copy-start | bytes 52
  8.0 533.0 %all-reduce.2.cloned.1.call-start = ((), (), s32[]{:S(2)}) async-start(), calls=%async_computation.2 | async-start | bytes 2097152 | tf_op jit(solution)/shard_map/psum | solution.py:101
  39.6 53.8 %collective-permute-start = (bf16[2048,512]{1,0:T(8,128)(2,1)S(1)}, bf16[2048,512]{1,0:T(8,128)(2,1)}, u32[]{:S(2)}, u32[]{:S(2)}) collective-permute-start(bf16[2048,512]{1,0:T(8,128)(2,1)S(1)} %bitcast.41), channel_id=1, source_target_pairs={{0,4},{4,8},{8,12},{12,16},{16,20},{20,24},{24,28},{28,32},{32,36}... | collective-permute-start | bytes 6291464 | tf_op jit(solution)/shard_map/ppermute | solution.py:16
  39.7 53.8 %collective-permute-start.2 = (bf16[2048,512]{1,0:T(8,128)(2,1)S(1)}, bf16[2048,512]{1,0:T(8,128)(2,1)}, u32[]{:S(2)}, u32[]{:S(2)}) collective-permute-start(bf16[2048,512]{1,0:T(8,128)(2,1)S(1)} %bitcast.42), channel_id=1, source_target_pairs={{0,252},{4,0},{8,4},{12,8},{16,12},{20,16},{24,20},{28,24},{32,28}... | collective-permute-start | bytes 6291464 | tf_op jit(solution)/shard_map/ppermute | solution.py:16
  93.5 51.6 %collective-permute-start.1 = (bf16[2048,512]{1,0:T(8,128)(2,1)}, bf16[2048,512]{1,0:T(8,128)(2,1)}, u32[]{:S(2)}, u32[]{:S(2)}) collective-permute-start(bf16[2048,512]{1,0:T(8,128)(2,1)} %collective-permute-done), channel_id=1, source_target_pairs={{0,4},{4,8},{8,12},{12,16},{16,20},{20,24},{24,28},{28,32},{32,36}... | collective-permute-start | bytes 6291464 | tf_op jit(solution)/shard_map/ppermute | solution.py:16
  93.5 56.9 %collective-permute-start.3 = (bf16[2048,512]{1,0:T(8,128)(2,1)}, bf16[2048,512]{1,0:T(8,128)(2,1)}, u32[]{:S(2)}, u32[]{:S(2)}) collective-permute-start(bf16[2048,512]{1,0:T(8,128)(2,1)} %collective-permute-done.2), channel_id=1, source_target_pairs={{0,252},{4,0},{8,4},{12,8},{16,12},{20,16},{24,20},{28,24},{32,28}... | collective-permute-start | bytes 6291464 | tf_op jit(solution)/shard_map/ppermute | solution.py:16
  152.2 4.0 copy-start.3
  156.2 7.0 %copy-start.2 = (bf16[4,8,128,128]{3,2,1,0:T(8,128)(2,1)S(1)}, bf16[4,8,128,128]{3,2,1,0:T(8,128)(2,1)}, u32[]{:S(2)}) copy-start(bf16[4,8,128,128]{3,2,1,0:T(8,128)(2,1)} %param.8) | copy-start | bytes 3145732
  163.1 3.0 copy-start.7
  166.2 2.1 copy-start.4
  211.6 45.0 %collective-permute-start.6 = (bf16[2048,512]{1,0:T(8,128)(2,1)}, bf16[2048,512]{1,0:T(8,128)(2,1)}, u32[]{:S(2)}, u32[]{:S(2)}) collective-permute-start(bf16[2048,512]{1,0:T(8,128)(2,1)} %bitcast.13), channel_id=1, source_target_pairs={{0,252},{4,0},{8,4},{12,8},{16,12},{20,16},{24,20},{28,24},{32,28}... | collective-permute-start | bytes 6291464 | tf_op jit(solution)/shard_map/ppermute | solution.py:16
  213.0 55.0 %collective-permute-start.4 = (bf16[2048,512]{1,0:T(8,128)(2,1)}, bf16[2048,512]{1,0:T(8,128)(2,1)}, u32[]{:S(2)}, u32[]{:S(2)}) collective-permute-start(bf16[2048,512]{1,0:T(8,128)(2,1)} %bitcast.11), channel_id=1, source_target_pairs={{0,4},{4,8},{8,12},{12,16},{16,20},{20,24},{24,28},{28,32},{32,36}... | collective-permute-start | bytes 6291464 | tf_op jit(solution)/shard_map/ppermute | solution.py:16
  261.5 48.7 %collective-permute-start.7 = (bf16[2048,512]{1,0:T(8,128)(2,1)}, bf16[2048,512]{1,0:T(8,128)(2,1)}, u32[]{:S(2)}, u32[]{:S(2)}) collective-permute-start(bf16[2048,512]{1,0:T(8,128)(2,1)} %fusion), channel_id=1, source_target_pairs={{0,252},{4,0},{8,4},{12,8},{16,12},{20,16},{24,20},{28,24},{32,28}... | collective-permute-start | bytes 6291464 | tf_op jit(solution)/shard_map/ppermute | solution.py:16
  268.1 4.1 copy-start.5
  272.1 50.1 %collective-permute-start.5 = (bf16[2048,512]{1,0:T(8,128)(2,1)}, bf16[2048,512]{1,0:T(8,128)(2,1)S(1)}, u32[]{:S(2)}, u32[]{:S(2)}) collective-permute-start(bf16[2048,512]{1,0:T(8,128)(2,1)} %fusion.1), channel_id=1, source_target_pairs={{0,4},{4,8},{8,12},{12,16},{16,20},{20,24},{24,28},{28,32},{32,36}... | collective-permute-start | bytes 6291464 | tf_op jit(solution)/shard_map/ppermute | solution.py:16
  273.6 269.8 %reduce-scatter.2.cloned.1.call-start = ((), (), s32[]{:S(2)}) async-start(), calls=%async_computation.3 | async-start | bytes 2621440 | tf_op jit(solution)/shard_map/reduce_scatter | solution.py:118
  322.3 221.1 %copy-start.1 = (bf16[512,512]{1,0:T(8,128)(2,1)S(1)}, bf16[512,512]{1,0:T(8,128)(2,1)}, u32[]{:S(2)}) copy-start(bf16[512,512]{1,0:T(8,128)(2,1)} %param.7) | copy-start | bytes 1572868
Sparse Core Ops, SparseCore 0:
  273.7 267.2 all-reduce.1
Sparse Core Ops, SparseCore 1:
  327.5 28.4 reduce-scatter.1
where the time goes:
time: 552 us; the launch traced here: 551 us
  waiting for transfers between devices  385 us (70%)
  other arithmetic  43.4 us (8%)
  local copies, waits for them, and re-layouts  41.5 us (8%)
  blocking collectives  30.3 us (5%)
  starting transfers between devices  24.1 us (4%)
  between operations  15.6 us (3%)
  matrix products  11.1 us (2%)
    psum x1, waiting for transfers between devices, local(): lax.psum(weight_term, ('blk', 'repl')) * (1.0 / math.sqrt(nodes_total))  214 us
    ppermute x8, waiting for transfers between devices, passed_along(): return lax.ppermute(value, axis, pairs)  171 us
    all_to_all x1, blocking collectives, from_everyone(): lax.all_to_all(jnp.broadcast_to(x[None], (length, *x.shape)), axis, 0, 0,...  30.3 us
    ppermute x8, starting transfers between devices, passed_along(): return lax.ppermute(value, axis, pairs)  24 us
    scatter-add x1, other arithmetic, local(): jax.ops.segment_sum(contrib.reshape(block_rows * SLOTS, TILE, feat_width)...  18.8 us
    slice x2, local copies, waits for them, and re-layouts, local(): shares = [panel_parts[position] for position in range(span_count)]  12.4 us
  transfers between devices with their start and end apart: 10, of which 6 were waited for; matrix products, arithmetic and copies ran while one was open for 6% of the time, Pallas kernels for 0%

commit v1 on v0

v1 whole, which is shorter than its diff:
```python
import functools
import math

import jax
import jax.numpy as jnp
from jax import lax
from jax.experimental import pallas as pl
from jax.experimental.pallas import tpu as pltpu
from jax.sharding import PartitionSpec as P

TILE = 128
SLOTS = 8
REACH = 2
SPAN = 2 * REACH + 1
GROUP = 4
MESH = pl.DeviceIdType.MESH
BF16 = jnp.bfloat16
F32 = jnp.float32
RUN = 8


def place(nb, run):
    b = lax.axis_index("blk")
    r = lax.axis_index("repl")
    flip = 2 * ((b // run) % 2)
    g = (r + flip) % GROUP
    up = (b + 1) % nb
    down = (b + nb - 1) % nb
    r_up = (g + 2 * ((up // run) % 2)) % GROUP
    r_down = (g + 2 * ((down // run) % 2)) % GROUP
    p1 = r + 1 - 2 * (r % 2)
    p2 = (r + 2) % GROUP
    p3 = (p1 + 2) % GROUP
    return b, r, flip, g, up, down, r_up, r_down, p1, p2, p3


def partners(r):
    p1 = r + 1 - 2 * (r % 2)
    return r, p1, (r + 2) % GROUP, (p1 + 2) % GROUP


def remote(src, dst, send, recv, b, r):
    return pltpu.make_async_remote_copy(
        src_ref=src, dst_ref=dst, send_sem=send, recv_sem=recv, device_id=(b, r), device_id_type=MESH
    )


def greet(peers):
    barrier = pltpu.get_barrier_semaphore()
    for peer in peers:
        pl.semaphore_signal(barrier, inc=1, device_id=peer, device_id_type=MESH)
    pl.semaphore_wait(barrier, len(peers))


def columns(ref, block):
    return ref.at[:, :, pl.ds(pl.multiple_of(block * TILE, TILE), TILE)]


def forward_kernel(
    nb, run,
    feats, weight, vals, table, cot,
    out, wterm, bt_all, vals_all, table_all,
    win, vbuf, tbuf, tsm, wv, cv, ov, aggs, aggr, slope, bts, wt,
    fs, fr, us, ur, ds_, dr, us2, ur2, ds2, dr2, vs, vr, ts, tr, asend, arecv, bsend, brecv, loc,
):
    b, r, flip, g, up, down, r_up, r_down, p1, p2, p3 = place(nb, run)
    greet([(b, p1), (b, p2), (b, p3), (up, r_up), (down, r_down)])

    def group_of(member):
        return (member + flip) % GROUP

    sends = []

    def go(copy):
        copy.start()
        sends.append(copy)

    rows = vals.shape[0]
    panel_blocks = GROUP * rows
    dead = SPAN * panel_blocks

    def piece(panel, member):
        return win.at[pl.ds(panel * panel_blocks + member * rows, rows)]

    mine = columns(feats, g)
    for slot, p in ((0, p2), (1, p3), (2, p1)):
        go(remote(columns(feats, group_of(p)), piece(2, r), fs.at[slot], fr.at[r], b, p))
    go(remote(mine, piece(1, r), us.at[0], ur.at[r], up, r_up))
    go(remote(mine, piece(3, r), ds_.at[0], dr.at[r], down, r_down))
    for slot, p in ((0, p2), (1, p3), (2, p1)):
        go(remote(table, tbuf.at[r], ts.at[slot], tr.at[r], b, p))
    for c in range(rows):
        go(remote(vals.at[c], vbuf.at[r, c], vs.at[0, c], vr.at[r, c], b, p2))
        go(remote(vals.at[c], vbuf.at[r, c], vs.at[1, c], vr.at[r, c], b, p1))
    own = [
        pltpu.make_async_copy(mine, piece(2, r), loc.at[0]),
        pltpu.make_async_copy(vals, vbuf.at[r], loc.at[1]),
        pltpu.make_async_copy(table, tbuf.at[r], loc.at[2]),
        pltpu.make_async_copy(weight, wv, loc.at[3]),
        pltpu.make_async_copy(cot, cv, loc.at[4]),
    ]
    for copy in own:
        copy.start()
    win[dead] = jnp.zeros((TILE, TILE), BF16)

    def landed(dst, recv):
        remote(dst, dst, fs.at[0], recv, b, p1).wait_recv()

    for slot, p in ((1, p1), (2, p2), (3, p3)):
        landed(piece(2, p), fr.at[p])
        go(remote(piece(2, p), piece(1, p), us.at[slot], ur.at[p], up, r_up))
        go(remote(piece(2, p), piece(3, p), ds_.at[slot], dr.at[p], down, r_down))
    from_below = partners(r_down)
    from_above = partners(r_up)
    for slot in range(GROUP):
        i = from_below[slot]
        landed(piece(1, i), ur.at[i])
        go(remote(piece(1, i), piece(0, i), us2.at[slot], ur2.at[i], up, r_up))
        i = from_above[slot]
        landed(piece(3, i), dr.at[i])
        go(remote(piece(3, i), piece(4, i), ds2.at[slot], dr2.at[i], down, r_down))
        if slot < rows:
            landed(vbuf.at[p2, slot], vr.at[p2, slot])
            go(remote(vbuf.at[p2, slot], vbuf.at[p2, slot], vs.at[2, slot], vr.at[p2, slot], b, p1))
    for i in range(GROUP):
        landed(piece(0, i), ur2.at[i])
        landed(piece(4, i), dr2.at[i])
    for p in (p1, p3):
        for c in range(rows):
            landed(vbuf.at[p, c], vr.at[p, c])
    for p in (p1, p2, p3):
        landed(tbuf.at[p], tr.at[p])
    for copy in own:
        copy.wait()
    to_scalars = pltpu.make_async_copy(tbuf, tsm, loc.at[0])
    to_scalars.start()
    keep = [
        pltpu.make_async_copy(vbuf, vals_all, loc.at[1]),
        pltpu.make_async_copy(tbuf, table_all, loc.at[2]),
    ]
    for copy in keep:
        copy.start()
    to_scalars.wait()

    for slot, q in ((0, p2), (1, p3), (2, p1), (3, r)):

        def one_row(kk, carry, q=q):
            left = [vbuf[q, kk, s] for s in range(SLOTS)]
            right = [win[tsm[q, 0, kk * SLOTS + s]] for s in range(SLOTS)]
            total = jnp.dot(
                jnp.concatenate(left, axis=1), jnp.concatenate(right, axis=0), preferred_element_type=F32
            )
            aggs[q, pl.ds(pl.multiple_of(kk * TILE, TILE), TILE), :] = total.astype(BF16)
            return carry

        lax.fori_loop(0, rows, one_row, 0)
        if slot < 3:
            go(remote(aggs.at[q], aggr.at[g], asend.at[slot], arecv.at[g], b, q))
        else:
            last = pltpu.make_async_copy(aggs.at[q], aggr.at[g], loc.at[0])
            last.start()
            last.wait()
    for p in (p1, p2, p3):
        gp = group_of(p)
        landed(aggr.at[gp], arecv.at[gp])

    def dense(t, carry):
        span = pl.ds(pl.multiple_of(t * TILE, TILE), TILE)
        agg = jnp.concatenate([aggr[i, span, :] for i in range(GROUP)], axis=1)
        pre = jnp.dot(agg, wv[...], preferred_element_type=F32)
        sigma = jax.nn.sigmoid(pre)
        ov[span, :] = (pre * sigma).astype(BF16)
        grad = cv[span, :].astype(F32) * (sigma * (1.0 + pre * (1.0 - sigma)))
        slope[span, :] = grad.astype(BF16)
        return carry

    lax.fori_loop(0, rows, dense, 0)
    tail = [pltpu.make_async_copy(ov, out, loc.at[3])]
    tail[0].start()
    for slot, q in ((0, p2), (1, p3), (2, p1), (3, r)):
        gq = group_of(q)
        part = wv[pl.ds(pl.multiple_of(gq * TILE, TILE), TILE), :]
        back = lax.dot_general(part, slope[...], (((1,), (1,)), ((), ())), preferred_element_type=F32)
        bts[q] = back.astype(BF16)
        if slot < 3:
            go(remote(bts.at[q], bt_all.at[r], bsend.at[slot], brecv.at[r], b, q))
        else:
            copy = pltpu.make_async_copy(bts.at[q], bt_all.at[r], loc.at[4])
            copy.start()
            tail.append(copy)
    for i in range(GROUP):
        wt[pl.ds(i * TILE, TILE), :] = lax.dot_general(
            aggr[i], slope[...], (((0,), (0,)), ((), ())), preferred_element_type=F32
        )
    copy = pltpu.make_async_copy(wt, wterm, loc.at[0])
    copy.start()
    tail.append(copy)
    for copy in keep + tail:
        copy.wait()
    for p in (p1, p2, p3):
        landed(bt_all.at[p], brecv.at[p])
    for copy in sends:
        copy.wait_send()


def scatter_kernel(rows, table, vals, bt, near, far, acc):
    k = pl.program_id(0)
    panel_blocks = GROUP * rows

    @pl.when(k == 0)
    def _():
        acc[...] = jnp.zeros_like(acc)

    tiles = jnp.concatenate([vals[0, 0, s] for s in range(SLOTS)], axis=1)
    terms = jnp.dot(bt[0], tiles, preferred_element_type=F32)
    for s in range(SLOTS):
        index = table[k // rows, 0, (k % rows) * SLOTS + s]
        acc[index] += terms[:, s * TILE : (s + 1) * TILE]

    @pl.when(k == panel_blocks - 1)
    def _():
        near[...] = acc[pl.ds(panel_blocks, 3 * panel_blocks)]
        far[0] = acc[pl.ds(0, panel_blocks)].astype(BF16)
        far[1] = acc[pl.ds(4 * panel_blocks, panel_blocks)].astype(BF16)


def return_kernel(
    nb, run, scale,
    near, far, wterm,
    grad, wgrad,
    ru2, rd2, su, sd, ru1, rd1, tot, rt, gv, a1, s1, a2, s2, a3, b3, b2, b1, wv,
    us, ur, ds_, dr, us2, ur2, ds2, dr2, ts, tr, w1s, w1r, w2s, w2r, w3s, w3r, x3s, x3r, x2s, x2r, x1s, x1r, loc,
):
    b, r, flip, g, up, down, r_up, r_down, p1, p2, p3 = place(nb, run)
    runs = nb // run
    m, z = b // run, b % run
    across = [((m + i) % runs) for i in range(1, runs)]
    along = [((z + i) % run) for i in range(1, run)]
    panel_peers = (p1, p2, p3)
    greet(
        [(b, p) for p in panel_peers]
        + [(up, r_up), (down, r_down)]
        + [(i * run + z, r) for i in across]
        + [(m * run + i, r) for i in along]
    )
    rows = gv.shape[0] // TILE
    sends = []

    def go(copy):
        copy.start()
        sends.append(copy)

    def landed(dst, recv):
        remote(dst, dst, ts.at[0], recv, b, p1).wait_recv()

    order = (p2, p3, p1, r)
    for slot, q in enumerate(order):
        block = pl.ds(q * rows, rows)
        go(remote(far.at[1, block], ru2.at[q], us.at[slot], ur.at[q], up, r_up))
        go(remote(far.at[0, block], rd2.at[q], ds_.at[slot], dr.at[q], down, r_down))
    quarter = wterm.shape[0] // GROUP
    for slot, q in enumerate((p2, p3, p1)):
        part = wterm.at[pl.ds(pl.multiple_of(q * quarter, quarter), quarter), :]
        go(remote(part, a1.at[r], w1s.at[slot], w1r.at[r], b, q))

    def relay(slot):
        q = partners_down[slot]
        landed(ru2.at[q], ur.at[q])
        su[q] = (ru2[q].astype(F32) + near[2, pl.ds(q * rows, rows)]).astype(BF16)
        go(remote(su.at[q], ru1.at[q], us2.at[slot], ur2.at[q], up, r_up))
        q = partners_up[slot]
        landed(rd2.at[q], dr.at[q])
        sd[q] = (rd2[q].astype(F32) + near[0, pl.ds(q * rows, rows)]).astype(BF16)
        go(remote(sd.at[q], rd1.at[q], ds2.at[slot], dr2.at[q], down, r_down))

    def ordered(member):
        a, c, d, e = partners(member)
        return d, e, c, a

    partners_down = ordered(r_down)
    partners_up = ordered(r_up)

    def finish(slot):
        q = order[slot]
        landed(ru1.at[q], ur2.at[q])
        landed(rd1.at[q], dr2.at[q])
        total = near[1, pl.ds(q * rows, rows)] + ru1[q].astype(F32) + rd1[q].astype(F32)
        tot[q] = total.astype(BF16)
        if slot < 3:
            go(remote(tot.at[q], rt.at[g], ts.at[slot], tr.at[g], b, q))
        else:
            rt[g] = tot[q]

    for slot in range(GROUP):
        relay(slot)
    for p in panel_peers:
        landed(a1.at[p], w1r.at[p])
    s1[...] = wterm[pl.ds(pl.multiple_of(r * quarter, quarter), quarter), :] + a1[p1] + (a1[p2] + a1[p3])
    piece = quarter // runs
    for slot, i in enumerate(across):
        part = s1.at[pl.ds(pl.multiple_of(i * piece, piece), piece), :]
        go(remote(part, a2.at[m], w2s.at[slot], w2r.at[m], i * run + z, r))
    finish(0)
    for i in across:
        landed(a2.at[i], w2r.at[i])
    total = s1[pl.ds(pl.multiple_of(m * piece, piece), piece), :]
    for i in across:
        total = total + a2[i]
    s2[...] = total
    tall = piece // (run // 4)

    def corner(ref, i):
        return ref.at[pl.ds(pl.multiple_of((i // 4) * tall, tall), tall), pl.ds(pl.multiple_of((i % 4) * TILE, TILE), TILE)]

    for slot, i in enumerate(along):
        go(remote(corner(s2, i), a3.at[z], w3s.at[slot], w3r.at[z], m * run + i, r))
    finish(1)
    for i in along:
        landed(a3.at[i], w3r.at[i])
    total = corner(s2, z)[...]
    for i in along:
        total = total + a3[i]
    corner(b3, z)[...] = total * scale
    for slot, i in enumerate(along):
        go(remote(corner(b3, z), corner(b3, z), x3s.at[slot], x3r.at[z], m * run + i, r))
    finish(2)
    for i in along:
        landed(corner(b3, i), x3r.at[i])
    b2[m] = b3[...].astype(BF16)
    for slot, i in enumerate(across):
        go(remote(b2.at[m], b2.at[m], x2s.at[slot], x2r.at[m], i * run + z, r))
    finish(3)
    for i in across:
        landed(b2.at[i], x2r.at[i])
    for slot, q in enumerate((p2, p3, p1)):
        go(remote(b2, b1.at[r], x1s.at[slot], x1r.at[r], b, q))
    b1[r] = b2[...]

    eye = (
        lax.broadcasted_iota(jnp.int32, (TILE, TILE), 0) == lax.broadcasted_iota(jnp.int32, (TILE, TILE), 1)
    ).astype(BF16)
    for p in panel_peers:
        gp = (p + flip) % GROUP
        landed(rt.at[gp], tr.at[gp])
    for i in range(GROUP):
        for t in range(rows):
            turned = lax.dot_general(eye, rt[i, t], (((1,), (1,)), ((), ())), preferred_element_type=F32)
            gv[pl.ds(t * TILE, TILE), pl.ds(i * TILE, TILE)] = turned.astype(BF16)
    done = pltpu.make_async_copy(gv, grad, loc.at[0])
    done.start()
    for p in panel_peers:
        landed(b1.at[p], x1r.at[p])
    for i in range(GROUP):
        for j in range(runs):
            wv[pl.ds(i * quarter + j * piece, piece), :] = b1[i, j].astype(F32)
    copy = pltpu.make_async_copy(wv, wgrad, loc.at[1])
    copy.start()
    done.wait()
    copy.wait()
    for copy in sends:
        copy.wait_send()


def window_table(tile_cols, tile_count, panel_blocks, nb):
    center = lax.axis_index("blk")
    offset = (tile_cols // panel_blocks - center) % nb
    offset = jnp.where(offset > REACH, offset - nb, offset)
    index = (offset + REACH) * panel_blocks + tile_cols % panel_blocks
    dead = SPAN * panel_blocks
    alive = jnp.arange(SLOTS, dtype=jnp.int32)[None, :] < tile_count[:, None]
    index = jnp.where(alive, jnp.clip(index, 0, dead - 1), dead).astype(jnp.int32)
    flat = index.reshape(1, -1)
    return jnp.pad(flat, ((0, 7), (0, TILE - flat.shape[1])))


def local(nb, run, feats, weight, vals, cols, count, cot):
    nodes, width = feats.shape
    rows = nodes // TILE
    panel_blocks = GROUP * rows
    runs = nb // run
    table = window_table(cols, count, panel_blocks, nb)
    anywhere = pl.BlockSpec(memory_space=pl.ANY)
    dma = pltpu.SemaphoreType.DMA
    shape = jax.ShapeDtypeStruct
    out, wterm, bt, vals_all, table_all = pl.pallas_call(
        functools.partial(forward_kernel, nb, run),
        out_shape=(
            shape((nodes, width), BF16),
            shape((width, width), F32),
            shape((GROUP, TILE, nodes), BF16),
            shape((GROUP, rows, SLOTS, TILE, TILE), BF16),
            shape((GROUP, 8, TILE), jnp.int32),
        ),
        in_specs=[anywhere] * 5,
        out_specs=(anywhere,) * 5,
        scratch_shapes=[
            pltpu.VMEM((SPAN * panel_blocks + 1, TILE, TILE), BF16),
            pltpu.VMEM((GROUP, rows, SLOTS, TILE, TILE), BF16),
            pltpu.VMEM((GROUP, 8, TILE), jnp.int32),
            pltpu.SMEM((GROUP, 8, TILE), jnp.int32),
            pltpu.VMEM((width, width), BF16),
            pltpu.VMEM((nodes, width), BF16),
            pltpu.VMEM((nodes, width), BF16),
            pltpu.VMEM((GROUP, nodes, TILE), BF16),
            pltpu.VMEM((GROUP, nodes, TILE), BF16),
            pltpu.VMEM((nodes, width), BF16),
            pltpu.VMEM((GROUP, TILE, nodes), BF16),
            pltpu.VMEM((width, width), F32),
            dma((3,)), dma((GROUP,)),
            dma((GROUP,)), dma((GROUP,)), dma((GROUP,)), dma((GROUP,)),
            dma((GROUP,)), dma((GROUP,)), dma((GROUP,)), dma((GROUP,)),
            dma((3, rows)), dma((GROUP, rows)),
            dma((3,)), dma((GROUP,)),
            dma((3,)), dma((GROUP,)),
            dma((3,)), dma((GROUP,)),
            dma((5,)),
        ],
        compiler_params=pltpu.CompilerParams(
            collective_id=0, has_side_effects=True, vmem_limit_bytes=60 << 20
        ),
        name="forward",
    )(feats.reshape(rows, TILE, width), weight, vals, table, cot)

    near, far = pl.pallas_call(
        functools.partial(scatter_kernel, rows),
        grid_spec=pltpu.PrefetchScalarGridSpec(
            num_scalar_prefetch=1,
            grid=(panel_blocks,),
            in_specs=[
                pl.BlockSpec((1, 1, SLOTS, TILE, TILE), lambda k, t: (k // rows, k % rows, 0, 0, 0)),
                pl.BlockSpec((1, TILE, TILE), lambda k, t: (k // rows, 0, k % rows)),
            ],
            out_specs=(
                pl.BlockSpec((3 * panel_blocks, TILE, TILE), lambda k, t: (0, 0, 0)),
                pl.BlockSpec((2, panel_blocks, TILE, TILE), lambda k, t: (0, 0, 0, 0)),
            ),
            scratch_shapes=[pltpu.VMEM((SPAN * panel_blocks + 1, TILE, TILE), F32)],
        ),
        out_shape=(
            shape((3 * panel_blocks, TILE, TILE), F32),
            shape((2, panel_blocks, TILE, TILE), BF16),
        ),
        compiler_params=pltpu.CompilerParams(
            dimension_semantics=("arbitrary",), vmem_limit_bytes=48 << 20
        ),
        name="scatter",
    )(table_all, vals_all, bt)

    chunk = (GROUP, rows, TILE, TILE)
    quarter = width // GROUP
    piece = quarter // runs
    tall = piece // (run // 4)
    in_vmem = pl.BlockSpec(memory_space=pltpu.VMEM)
    grad, wgrad = pl.pallas_call(
        functools.partial(return_kernel, nb, run, 1.0 / math.sqrt(nodes * GROUP * nb)),
        out_shape=(shape((nodes, width), BF16), shape((width, width), F32)),
        in_specs=[in_vmem, in_vmem, in_vmem],
        out_specs=(anywhere, anywhere),
        scratch_shapes=[
            pltpu.VMEM(chunk, BF16), pltpu.VMEM(chunk, BF16),
            pltpu.VMEM(chunk, BF16), pltpu.VMEM(chunk, BF16),
            pltpu.VMEM(chunk, BF16), pltpu.VMEM(chunk, BF16),
            pltpu.VMEM(chunk, BF16), pltpu.VMEM(chunk, BF16),
            pltpu.VMEM((nodes, width), BF16),
            pltpu.VMEM((GROUP, quarter, width), F32),
            pltpu.VMEM((quarter, width), F32),
            pltpu.VMEM((runs, piece, width), F32),
            pltpu.VMEM((piece, width), F32),
            pltpu.VMEM((run, tall, TILE), F32),
            pltpu.VMEM((piece, width), F32),
            pltpu.VMEM((runs, piece, width), BF16),
            pltpu.VMEM((GROUP, runs, piece, width), BF16),
            pltpu.VMEM((width, width), F32),
        ]
        + [dma((GROUP,))] * 10
        + [dma((3,)), dma((GROUP,))]
        + [dma((runs,)), dma((runs,))]
        + [dma((run,)), dma((run,))]
        + [dma((run,)), dma((run,))]
        + [dma((runs,)), dma((runs,))]
        + [dma((3,)), dma((GROUP,))]
        + [dma((2,))],
        compiler_params=pltpu.CompilerParams(
            collective_id=1, has_side_effects=True, vmem_limit_bytes=48 << 20
        ),
        name="giveback",
    )(near.reshape(3, panel_blocks, TILE, TILE), far, wterm)
    return out, wgrad, grad


def solution(mesh, run=RUN):
    both = ("blk", "repl")
    in_specs = (
        P(both, None),
        P(),
        P(both, None, None, None),
        P(both, None),
        P(both),
        P(both, None),
    )
    out_specs = (P(both, None), P(), P(both, None))
    body = functools.partial(local, mesh.shape["blk"], run)
    return jax.shard_map(body, mesh=mesh, in_specs=in_specs, out_specs=out_specs, check_vma=False)
```

time: 552 us -> 134 us (0.24)
  waiting for transfers between devices: 385 us -> 0 us
  Pallas kernels: 0 us -> 125 us
  other arithmetic: 43.4 us -> 0.76 us
  local copies, waits for them, and re-layouts: 41.5 us -> 6.73 us
  blocking collectives: 30.3 us -> 0 us
  starting transfers between devices: 24.1 us -> 0 us
  between operations: 15.6 us -> 0.7 us
  matrix products: 11.1 us -> 0 us
    psum x1 -> x0, waiting for transfers between devices: 214 us -> none  [local(): lax.psum(weight_term, ('blk', 'repl')) * (1.0 / math.sqrt(nodes_total))]
    ppermute x8 -> x0, waiting for transfers between devices: 171 us -> none  [passed_along(): return lax.ppermute(value, axis, pairs)]
    pallas_call x0 -> x3, Pallas kernels: none -> 125 us  [the longest x1 60.1 us: local(): pl.pallas_call(functools.partial(forward_kernel, nb, run), out_shape=(sha...]
    all_to_all x1 -> x0, blocking collectives: 30.3 us -> none  [from_everyone(): lax.all_to_all(jnp.broadcast_to(x[None], (length, *x.shape)), axis, 0, 0,...]
    ppermute x8 -> x0, starting transfers between devices: 24 us -> none  [passed_along(): return lax.ppermute(value, axis, pairs)]
    scatter-add x1 -> x0, other arithmetic: 18.8 us -> none  [local(): jax.ops.segment_sum(contrib.reshape(block_rows * SLOTS, TILE, feat_width)...]
    convert_element_type x3 -> x0, other arithmetic: 14.2 us -> none  [the longest x2 9 us: shortened(): a.astype(jnp.bfloat16)]
    slice x2 -> x0, local copies, waits for them, and re-layouts: 12.4 us -> none  [local(): shares = [panel_parts[position] for position in range(span_count)]]
  transfers between devices with their start and end apart: 10 -> 0, of which waited for: 6 -> 0; matrix products, arithmetic and copies ran while one was open for 6% -> 0% of each run, Pallas kernels for 0% -> 0%
where the time goes in v1:
time: 134 us; the launch traced here: 133 us
  Pallas kernels  125 us (93%)
  local copies, waits for them, and re-layouts  6.73 us (5%)
    pallas_call x1, Pallas kernels, local(): pl.pallas_call(functools.partial(forward_kernel, nb, run), out_shape=(sha...  60.1 us
    pallas_call x1, Pallas kernels, local(): pl.pallas_call(functools.partial(return_kernel, nb, run, 1.0 / math.sqrt(...  53.2 us
    pallas_call x1, Pallas kernels, local(): pl.pallas_call(functools.partial(scatter_kernel, rows), grid_spec=pltpu.P...  11.5 us
    unnamed x13, local copies, waits for them, and re-layouts  6.04 us

profile of v1, /device:TPU:1, one launch (start us, length us, event | category | flops | bytes accessed | tf_op | source)
XLA Modules:
  0.0 133.0 jit_solution(4098495945365568295)
XLA Ops:
  0.6 0.8 fusion.4
  1.4 0.1 reshape.17
  1.5 0.6 pad.4.table
  2.1 60.1 %forward.1 = (bf16[512,512]{1,0:T(8,128)(2,1)}, f32[512,512]{1,0:T(8,128)}, bf16[4,128,512]{2,1,0:T(8,128)(2,1)}, bf16[4,4,8,128,128]{4,3,2,1,0:T(8,128)(2,1)}, s32[4,8,128]{2,1,0:T(8,128)}) custom-call(bf16[4,128,512]{2,1,0:T(8,128)(2,1)} %bitcast.3, bf16[512,512]{1,0:T(8,128)(2,1)} %weight.1, bf16[4,8,128,128]{3,2,1,0:T(8,128)(2,1)} %vals.1, ...), custom_call_target="tpu_custom_call" | custom-call | tf_op jit(solution)/shard_map/forward/pallas_call | solution.py:385
  62.2 0.0 copy-start.1
  62.2 0.0 copy-start.2
  62.2 1.1 copy-done.2
  63.3 0.0 copy-start.3
  63.3 0.7 copy-done.3
  64.1 0.0 copy-start.4
  64.1 11.5 %scatter.1 = (f32[48,128,128]{2,1,0:T(8,128)S(1)}, bf16[2,16,128,128]{3,2,1,0:T(8,128)(2,1)S(1)}) custom-call(s32[4,8,128]{2,1,0:T(8,128)S(1)} %copy-done.3, bf16[4,4,8,128,128]{4,3,2,1,0:T(8,128)(2,1)} %get-tuple-element.14.vals, bf16[4,128,512]{2,1,0:T(8,128)(2,1)S(1)} %copy-done.2), custom_call_target="tpu_custom_call" | custom-call | tf_op jit(solution)/shard_map/scatter/pallas_call | solution.py:424
  75.6 0.0 copy-start
  75.6 1.6 %copy-done = f32[48,128,128]{2,1,0:T(8,128)} copy-done((f32[48,128,128]{2,1,0:T(8,128)}, f32[48,128,128]{2,1,0:T(8,128)S(1)}, u32[]{:S(2)}) %copy-start) | copy-done | bytes 3145752
  77.2 0.0 copy-done.1
  77.2 53.2 %giveback.1 = (bf16[512,512]{1,0:T(8,128)(2,1)S(1)}, f32[512,512]{1,0:T(8,128)S(1)}) custom-call(f32[3,16,128,128]{3,2,1,0:T(8,128)} %bitcast.2, bf16[2,16,128,128]{3,2,1,0:T(8,128)(2,1)S(1)} %get-tuple-element.17.far, f32[512,512]{1,0:T(8,128)S(1)} %copy-done.1), custom_call_target="tpu_custom_call" | custom-call | tf_op jit(solution)/shard_map/giveback/pallas_call | solution.py:454
  130.5 0.0 copy-done.4
  130.5 0.8 copy.12
  131.3 1.0 copy.13
  132.2 0.8 copy.14
Async XLA Ops:
  62.2 15.0 %copy-start.1 = (f32[512,512]{1,0:T(8,128)S(1)}, f32[512,512]{1,0:T(8,128)}, u32[]{:S(2)}) copy-start(f32[512,512]{1,0:T(8,128)} %get-tuple-element.18.wterm) | copy-start | bytes 3145732
  62.2 1.1 copy-start.2
  63.3 0.7 copy-start.3
  64.1 66.4 %copy-start.4 = (bf16[512,512]{1,0:T(8,128)(2,1)S(1)}, bf16[512,512]{1,0:T(8,128)(2,1)}, u32[]{:S(2)}) copy-start(bf16[512,512]{1,0:T(8,128)(2,1)} %get-tuple-element.24) | copy-start | bytes 1572868
  75.6 1.6 %copy-start = (f32[48,128,128]{2,1,0:T(8,128)}, f32[48,128,128]{2,1,0:T(8,128)S(1)}, u32[]{:S(2)}) copy-start(f32[48,128,128]{2,1,0:T(8,128)S(1)} %get-tuple-element.16) | copy-start | bytes 9437188

commit v2 on v1

v2 whole, which is shorter than its diff:
```python
import functools
import math

import jax
import jax.numpy as jnp
from jax import lax
from jax.experimental import pallas as pl
from jax.experimental.pallas import tpu as pltpu
from jax.sharding import PartitionSpec as P

TILE = 128
SLOTS = 8
REACH = 2
SPAN = 2 * REACH + 1
GROUP = 4
MESH = pl.DeviceIdType.MESH
BF16 = jnp.bfloat16
F32 = jnp.float32
RUN = 8


def place(nb, run):
    b = lax.axis_index("blk")
    r = lax.axis_index("repl")
    flip = 2 * ((b // run) % 2)
    g = (r + flip) % GROUP
    up = (b + 1) % nb
    down = (b + nb - 1) % nb
    r_up = (g + 2 * ((up // run) % 2)) % GROUP
    r_down = (g + 2 * ((down // run) % 2)) % GROUP
    p1 = r + 1 - 2 * (r % 2)
    p2 = (r + 2) % GROUP
    p3 = (p1 + 2) % GROUP
    return b, r, flip, g, up, down, r_up, r_down, p1, p2, p3


def partners(r):
    p1 = r + 1 - 2 * (r % 2)
    return r, p1, (r + 2) % GROUP, (p1 + 2) % GROUP


def remote(src, dst, send, recv, b, r):
    return pltpu.make_async_remote_copy(
        src_ref=src, dst_ref=dst, send_sem=send, recv_sem=recv, device_id=(b, r), device_id_type=MESH
    )


def greet(peers):
    barrier = pltpu.get_barrier_semaphore()
    for peer in peers:
        pl.semaphore_signal(barrier, inc=1, device_id=peer, device_id_type=MESH)
    pl.semaphore_wait(barrier, len(peers))


def ordered(member):
    own, core, chip, both = partners(member)
    return chip, both, core, own


def columns(ref, block):
    return ref.at[:, :, pl.ds(pl.multiple_of(block * TILE, TILE), TILE)]


def sorted_entries(dest):
    rows = lax.broadcasted_iota(jnp.int32, (TILE, TILE), 0)
    lanes = lax.broadcasted_iota(jnp.int32, (TILE, TILE), 1)
    across = jnp.broadcast_to(dest, (TILE, TILE))

    def count(mask, axis, value=1):
        return jnp.sum(jnp.where(mask, value, 0), axis=axis, keepdims=True)

    down = jnp.broadcast_to(count(rows == lanes, 1, across), (TILE, TILE))
    tie = (across == down) & (lanes < rows)
    rank = jnp.broadcast_to(count((across < down) | tie, 1), (TILE, TILE))
    repeat = jnp.broadcast_to(count(tie, 1), (TILE, TILE)) > 0
    hit = rank == lanes
    order = count(hit, 0, rows)
    before = jnp.where(count(hit & repeat, 0) > 0, lanes[0:1, :] - 1, TILE)
    owner = count(hit, 0, rows // SLOTS)
    upto = count(down <= lanes, 0)
    last = jnp.where(count(down == lanes, 0) > 0, upto - 1, TILE)
    return order, before, owner, last


def layer_kernel(
    nb, run, scale,
    feats, weight, vals, table, cot,
    out, grad, wgrad,
    win, vbuf, tbuf, smv, tsm, wv, cv, ov, aggs, aggr, slope, bts, btp, wt, runs,
    far, su, sd, ru2, rd2, ru1, rd1, tot, rt, gv, a1, s1, a2, s2, a3, b3, b2, b1, gw,
    fs, fr, us, ur, ds_, dr, us2, ur2, ds2, dr2, vs, vr, ts, tr, asend, arecv, bsend, brecv,
    vus, vur, vds, vdr, vus2, vur2, vds2, vdr2, gs, gr,
    w1s, w1r, w2s, w2r, w3s, w3r, x3s, x3r, x2s, x2r, x1s, x1r, loc,
):
    b, r, flip, g, up, down, r_up, r_down, p1, p2, p3 = place(nb, run)
    lines = nb // run
    m, z = b // run, b % run
    across = [((m + i) % lines) for i in range(1, lines)]
    along = [((z + i) % run) for i in range(1, run)]
    panel_peers = (p1, p2, p3)
    order = (p2, p3, p1, r)
    greet(
        [(b, p) for p in panel_peers]
        + [(up, r_up), (down, r_down)]
        + [(i * run + z, r) for i in across]
        + [(m * run + i, r) for i in along]
    )

    def group_of(member):
        return (member + flip) % GROUP

    sends = []

    def go(copy):
        copy.start()
        sends.append(copy)

    def landed(dst, recv):
        remote(dst, dst, fs.at[0], recv, b, p1).wait_recv()

    rows = vals.shape[0]
    panel_blocks = GROUP * rows
    dead = SPAN * panel_blocks

    def piece(panel, member):
        return win.at[pl.ds(panel * panel_blocks + member * rows, rows)]

    def tiles(member, c):
        return vbuf.at[pl.ds((member * rows + c) * SLOTS, SLOTS)]

    mine = columns(feats, g)
    for slot, p in enumerate((p2, p3, p1)):
        go(remote(columns(feats, group_of(p)), piece(2, r), fs.at[slot], fr.at[r], b, p))
    go(remote(mine, piece(1, r), us.at[0], ur.at[r], up, r_up))
    go(remote(mine, piece(3, r), ds_.at[0], dr.at[r], down, r_down))
    for slot, p in enumerate((p2, p3, p1)):
        go(remote(table, tbuf.at[r], ts.at[slot], tr.at[r], b, p))
    for c in range(rows):
        go(remote(vals.at[c], tiles(r, c), vs.at[0, c], vr.at[r, c], b, p2))
        go(remote(vals.at[c], tiles(r, c), vs.at[1, c], vr.at[r, c], b, p1))
    own = [
        pltpu.make_async_copy(table, tbuf.at[r], loc.at[0]),
        pltpu.make_async_copy(mine, piece(2, r), loc.at[1]),
        pltpu.make_async_copy(weight, wv, loc.at[2]),
        pltpu.make_async_copy(cot, cv, loc.at[3]),
    ] + [pltpu.make_async_copy(vals.at[c], tiles(r, c), loc.at[4 + c]) for c in range(rows)]
    for copy in own:
        copy.start()
    win[dead] = jnp.zeros((TILE, TILE), BF16)
    runs[TILE] = jnp.zeros((TILE, TILE), F32)

    for slot, p in ((1, p1), (2, p2), (3, p3)):
        landed(piece(2, p), fr.at[p])
        go(remote(piece(2, p), piece(1, p), us.at[slot], ur.at[p], up, r_up))
        go(remote(piece(2, p), piece(3, p), ds_.at[slot], dr.at[p], down, r_down))
    for p in panel_peers:
        landed(tbuf.at[p], tr.at[p])
    own[0].wait()
    dest = (tbuf[0] + tbuf[1]) + (tbuf[2] + tbuf[3])
    smv[0] = dest
    for line, value in enumerate(sorted_entries(dest[0:1, :])):
        smv[line + 1] = jnp.broadcast_to(value, (8, TILE))
    to_scalars = pltpu.make_async_copy(smv, tsm, loc.at[0])
    to_scalars.start()

    from_below = partners(r_down)
    from_above = partners(r_up)
    for slot in range(GROUP):
        i = from_below[slot]
        landed(piece(1, i), ur.at[i])
        go(remote(piece(1, i), piece(0, i), us2.at[slot], ur2.at[i], up, r_up))
        i = from_above[slot]
        landed(piece(3, i), dr.at[i])
        go(remote(piece(3, i), piece(4, i), ds2.at[slot], dr2.at[i], down, r_down))
        if slot < rows:
            landed(tiles(p2, slot), vr.at[p2, slot])
            go(remote(tiles(p2, slot), tiles(p2, slot), vs.at[2, slot], vr.at[p2, slot], b, p1))
    for i in range(GROUP):
        landed(piece(0, i), ur2.at[i])
        landed(piece(4, i), dr2.at[i])
    for copy in own[1:]:
        copy.wait()
    to_scalars.wait()
    for p in (p1, p3):
        for c in range(rows):
            landed(tiles(p, c), vr.at[p, c])

    for slot, q in enumerate(order):

        def one_row(kk, carry, q=q):
            first = (q * rows + kk) * SLOTS
            left = [vbuf[first + s] for s in range(SLOTS)]
            right = [win[tsm[0, 0, first + s]] for s in range(SLOTS)]
            total = jnp.dot(
                jnp.concatenate(left, axis=1), jnp.concatenate(right, axis=0), preferred_element_type=F32
            )
            aggs[q, pl.ds(pl.multiple_of(kk * TILE, TILE), TILE), :] = total.astype(BF16)
            return carry

        lax.fori_loop(0, rows, one_row, 0)
        if slot < 3:
            go(remote(aggs.at[q], aggr.at[g], asend.at[slot], arecv.at[g], b, q))
        else:
            last = pltpu.make_async_copy(aggs.at[q], aggr.at[g], loc.at[0])
            last.start()
            last.wait()
    for p in panel_peers:
        gp = group_of(p)
        landed(aggr.at[gp], arecv.at[gp])

    def dense(t, carry):
        span = pl.ds(pl.multiple_of(t * TILE, TILE), TILE)
        agg = jnp.concatenate([aggr[i, span, :] for i in range(GROUP)], axis=1)
        pre = jnp.dot(agg, wv[...], preferred_element_type=F32)
        sigma = jax.nn.sigmoid(pre)
        ov[span, :] = (pre * sigma).astype(BF16)
        slant = cv[span, :].astype(F32) * (sigma * (1.0 + pre * (1.0 - sigma)))
        slope[span, :] = slant.astype(BF16)
        return carry

    lax.fori_loop(0, rows, dense, 0)
    ends = [pltpu.make_async_copy(ov, out, loc.at[1])]
    ends[0].start()

    def back_rows(q):
        part = wv[pl.ds(pl.multiple_of(group_of(q) * TILE, TILE), TILE), :]
        for t in range(rows):
            turned = lax.dot_general(
                part, slope[pl.ds(t * TILE, TILE), :], (((1,), (1,)), ((), ())), preferred_element_type=F32
            )
            yield t, turned.astype(BF16)

    for slot, q in enumerate(order):
        for t, value in back_rows(q):
            if slot < 3:
                bts[slot, t] = value
            else:
                btp[r * rows + t] = value
        if slot < 3:
            go(remote(bts.at[slot], btp.at[pl.ds(r * rows, rows)], bsend.at[slot], brecv.at[r], b, q))
    for slot, q in enumerate(order):
        wt[q] = lax.dot_general(aggr[q], slope[...], (((0,), (0,)), ((), ())), preferred_element_type=F32)
        if slot < 3:
            go(remote(wt.at[q], a1.at[r], w1s.at[slot], w1r.at[r], b, q))
    for p in panel_peers:
        landed(btp.at[pl.ds(p * rows, rows)], brecv.at[p])

    def eight(t, carry):
        first = t * 8
        terms = [
            jnp.dot(btp[tsm[3, 0, first + i]], vbuf[tsm[1, 0, first + i]], preferred_element_type=F32)
            for i in range(8)
        ]
        for i in range(8):
            runs[first + i] = terms[i] + runs[tsm[2, 0, first + i]]
        return carry

    lax.fori_loop(0, panel_blocks * SLOTS // 8, eight, 0)

    def share(panel, q, t):
        return runs[tsm[4, 0, panel * panel_blocks + q * rows + t]]

    for slot, q in enumerate(order):
        for t in range(rows):
            far[0, q, t] = share(4, q, t).astype(BF16)
            far[1, q, t] = share(0, q, t).astype(BF16)
        go(remote(far.at[0, q], ru2.at[q], vus.at[slot], vur.at[q], up, r_up))
        go(remote(far.at[1, q], rd2.at[q], vds.at[slot], vdr.at[q], down, r_down))

    order_below = ordered(r_down)
    order_above = ordered(r_up)

    def relay(slot):
        q = order_below[slot]
        landed(ru2.at[q], vur.at[q])
        for t in range(rows):
            su[q, t] = (ru2[q, t].astype(F32) + share(3, q, t)).astype(BF16)
        go(remote(su.at[q], ru1.at[q], vus2.at[slot], vur2.at[q], up, r_up))
        q = order_above[slot]
        landed(rd2.at[q], vdr.at[q])
        for t in range(rows):
            sd[q, t] = (rd2[q, t].astype(F32) + share(1, q, t)).astype(BF16)
        go(remote(sd.at[q], rd1.at[q], vds2.at[slot], vdr2.at[q], down, r_down))

    def finish(slot):
        q = order[slot]
        landed(ru1.at[q], vur2.at[q])
        landed(rd1.at[q], vdr2.at[q])
        for t in range(rows):
            total = share(2, q, t) + (ru1[q, t].astype(F32) + rd1[q, t].astype(F32))
            if slot < 3:
                tot[q, t] = total.astype(BF16)
            else:
                rt[g, t] = total.astype(BF16)
        if slot < 3:
            go(remote(tot.at[q], rt.at[g], gs.at[slot], gr.at[g], b, q))

    quarter = wt.shape[1]
    part = quarter // lines
    tall = part // (run // 4)

    def corner(ref, i):
        return ref.at[pl.ds(pl.multiple_of((i // 4) * tall, tall), tall), pl.ds(pl.multiple_of((i % 4) * TILE, TILE), TILE)]

    relay(0)
    relay(1)
    for p in panel_peers:
        landed(a1.at[p], w1r.at[p])
    s1[...] = wt[r] + a1[p1] + (a1[p2] + a1[p3])
    for slot, i in enumerate(across):
        chunk = s1.at[pl.ds(pl.multiple_of(i * part, part), part), :]
        go(remote(chunk, a2.at[m], w2s.at[slot], w2r.at[m], i * run + z, r))
    relay(2)
    relay(3)
    for i in across:
        landed(a2.at[i], w2r.at[i])
    total = s1[pl.ds(pl.multiple_of(m * part, part), part), :]
    for i in across:
        total = total + a2[i]
    s2[...] = total
    for slot, i in enumerate(along):
        go(remote(corner(s2, i), a3.at[z], w3s.at[slot], w3r.at[z], m * run + i, r))
    finish(0)
    for i in along:
        landed(a3.at[i], w3r.at[i])
    total = corner(s2, z)[...]
    for i in along:
        total = total + a3[i]
    corner(b3, z)[...] = total * scale
    for slot, i in enumerate(along):
        go(remote(corner(b3, z), corner(b3, z), x3s.at[slot], x3r.at[z], m * run + i, r))
    finish(1)
    for i in along:
        landed(corner(b3, i), x3r.at[i])
    b2[m] = b3[...].astype(BF16)
    for slot, i in enumerate(across):
        go(remote(b2.at[m], b2.at[m], x2s.at[slot], x2r.at[m], i * run + z, r))
    finish(2)
    for i in across:
        landed(b2.at[i], x2r.at[i])
    for slot, q in enumerate((p2, p3, p1)):
        go(remote(b2, b1.at[r], x1s.at[slot], x1r.at[r], b, q))
    b1[r] = b2[...]
    finish(3)

    eye = (
        lax.broadcasted_iota(jnp.int32, (TILE, TILE), 0) == lax.broadcasted_iota(jnp.int32, (TILE, TILE), 1)
    ).astype(BF16)
    for p in panel_peers:
        gp = group_of(p)
        landed(rt.at[gp], gr.at[gp])
    for i in range(GROUP):
        for t in range(rows):
            turned = lax.dot_general(eye, rt[i, t], (((1,), (1,)), ((), ())), preferred_element_type=F32)
            gv[pl.ds(t * TILE, TILE), pl.ds(i * TILE, TILE)] = turned.astype(BF16)
    ends.append(pltpu.make_async_copy(gv, grad, loc.at[2]))
    ends[-1].start()
    for p in panel_peers:
        landed(b1.at[p], x1r.at[p])
    for i in range(GROUP):
        for j in range(lines):
            gw[pl.ds(i * quarter + j * part, part), :] = b1[i, j].astype(F32)
    ends.append(pltpu.make_async_copy(gw, wgrad, loc.at[3]))
    ends[-1].start()
    for copy in ends:
        copy.wait()
    for copy in sends:
        copy.wait_send()


def window_table(tile_cols, tile_count, panel_blocks, nb):
    center = lax.axis_index("blk")
    offset = (tile_cols // panel_blocks - center) % nb
    offset = jnp.where(offset > REACH, offset - nb, offset)
    index = (offset + REACH) * panel_blocks + tile_cols % panel_blocks
    dead = SPAN * panel_blocks
    alive = jnp.arange(SLOTS, dtype=jnp.int32)[None, :] < tile_count[:, None]
    index = jnp.where(alive, jnp.clip(index, 0, dead - 1), dead).astype(jnp.int32)
    line = jnp.tile(index.reshape(1, -1), (8, GROUP))
    lane = lax.broadcasted_iota(jnp.int32, line.shape, 1)
    return jnp.where(lane // index.size == lax.axis_index("repl"), line, 0)


def local(nb, run, feats, weight, vals, cols, count, cot):
    nodes, width = feats.shape
    rows = nodes // TILE
    panel_blocks = GROUP * rows
    lines = nb // run
    table = window_table(cols, count, panel_blocks, nb)
    anywhere = pl.BlockSpec(memory_space=pl.ANY)
    dma = pltpu.SemaphoreType.DMA
    shape = jax.ShapeDtypeStruct
    chunk = (GROUP, rows, TILE, TILE)
    quarter = width // GROUP
    part = quarter // lines
    tall = part // (run // 4)
    pair = [dma((GROUP,)), dma((GROUP,))]
    out, grad, wgrad = pl.pallas_call(
        functools.partial(layer_kernel, nb, run, 1.0 / math.sqrt(nodes * GROUP * nb)),
        out_shape=(
            shape((nodes, width), BF16),
            shape((nodes, width), BF16),
            shape((width, width), F32),
        ),
        in_specs=[anywhere] * 5,
        out_specs=(anywhere,) * 3,
        scratch_shapes=[
            pltpu.VMEM((SPAN * panel_blocks + 1, TILE, TILE), BF16),
            pltpu.VMEM((panel_blocks * SLOTS, TILE, TILE), BF16),
            pltpu.VMEM((GROUP, 8, TILE), jnp.int32),
            pltpu.VMEM((5, 8, TILE), jnp.int32),
            pltpu.SMEM((5, 8, TILE), jnp.int32),
            pltpu.VMEM((width, width), BF16),
            pltpu.VMEM((nodes, width), BF16),
            pltpu.VMEM((nodes, width), BF16),
            pltpu.VMEM((GROUP, nodes, TILE), BF16),
            pltpu.VMEM((GROUP, nodes, TILE), BF16),
            pltpu.VMEM((nodes, width), BF16),
            pltpu.VMEM((GROUP - 1, rows, TILE, TILE), BF16),
            pltpu.VMEM((panel_blocks, TILE, TILE), BF16),
            pltpu.VMEM((GROUP, quarter, width), F32),
            pltpu.VMEM((panel_blocks * SLOTS + 1, TILE, TILE), F32),
            pltpu.VMEM((2,) + chunk, BF16),
        ]
        + [pltpu.VMEM(chunk, BF16)] * 8
        + [
            pltpu.VMEM((nodes, width), BF16),
            pltpu.VMEM((GROUP, quarter, width), F32),
            pltpu.VMEM((quarter, width), F32),
            pltpu.VMEM((lines, part, width), F32),
            pltpu.VMEM((part, width), F32),
            pltpu.VMEM((run, tall, TILE), F32),
            pltpu.VMEM((part, width), F32),
            pltpu.VMEM((lines, part, width), BF16),
            pltpu.VMEM((GROUP, lines, part, width), BF16),
            pltpu.VMEM((width, width), F32),
        ]
        + pair * 5
        + [dma((3, rows)), dma((GROUP, rows))]
        + pair * 3
        + pair * 5
        + pair
        + [dma((lines,)), dma((lines,))]
        + [dma((run,)), dma((run,))] * 2
        + [dma((lines,)), dma((lines,))]
        + pair
        + [dma((8,))],
        compiler_params=pltpu.CompilerParams(
            collective_id=0, has_side_effects=True, vmem_limit_bytes=62 << 20
        ),
        name="layer",
    )(feats.reshape(rows, TILE, width), weight, vals, table, cot)
    return out, wgrad, grad


def solution(mesh, run=RUN):
    both = ("blk", "repl")
    in_specs = (
        P(both, None),
        P(),
        P(both, None, None, None),
        P(both, None),
        P(both),
        P(both, None),
    )
    out_specs = (P(both, None), P(), P(both, None))
    body = functools.partial(local, mesh.shape["blk"], run)
    return jax.shard_map(body, mesh=mesh, in_specs=in_specs, out_specs=out_specs, check_vma=False)
```

time: 134 us -> 121 us (0.903)
  Pallas kernels: 125 us -> 114 us
  local copies, waits for them, and re-layouts: 6.73 us -> 5 us
    pallas_call x3 -> x1, Pallas kernels: 125 us -> 114 us  [local(): pl.pallas_call(functools.partial(layer_kernel, nb, run, 1.0 / math.sqrt(n...]
    unnamed x13 -> x11, local copies, waits for them, and re-layouts: 6.04 us -> 4.82 us
where the time goes in v2:
time: 121 us
  Pallas kernels  114 us (94%)
  local copies, waits for them, and re-layouts  5 us (4%)
    pallas_call x1, Pallas kernels, local(): pl.pallas_call(functools.partial(layer_kernel, nb, run, 1.0 / math.sqrt(n...  114 us
    unnamed x11, local copies, waits for them, and re-layouts  4.82 us

profile of v2, /device:TPU:1, one launch (start us, length us, event | category | flops | bytes accessed | tf_op | source)
XLA Modules:
  0.0 120.9 jit_solution(4899755654651379949)
XLA Ops:
  0.7 0.0 copy-start.2
  0.7 0.0 copy-start.3
  0.7 0.7 copy-done.2
  1.3 0.0 copy-done.3
  1.3 0.1 fusion.5
  1.4 0.1 tile.12
  1.5 0.1 tile.14
  1.6 0.6 fusion.table
  2.2 114.5 %layer.1 = (bf16[512,512]{1,0:T(8,128)(2,1)}, bf16[512,512]{1,0:T(8,128)(2,1)}, f32[512,512]{1,0:T(8,128)}) custom-call(bf16[4,128,512]{2,1,0:T(8,128)(2,1)} %bitcast.1, bf16[512,512]{1,0:T(8,128)(2,1)} %weight.1, bf16[4,8,128,128]{3,2,1,0:T(8,128)(2,1)} %vals.1, s32[8,128]{1,0:T(8,128)} %fusion.table, bf16[512,512]{1,0:T(8,128)(2,1)} %cot.1), custom_call_target="tpu_custom_call" | custom-call | tf_op jit(solution)/shard_map/layer/pallas_call | solution.py:398
  116.7 0.0 copy-start
  116.7 2.0 %copy.12 = bf16[512,512]{1,0:T(8,128)(2,1)} copy(bf16[512,512]{1,0:T(8,128)(2,1)} %get-tuple-element.14) | data formatting | bytes 1048576
  118.7 0.0 copy-done
  118.7 0.0 copy-start.1
  118.7 1.0 copy.13
  119.6 0.4 copy-done.1
  120.1 0.8 copy.14
  (3 shorter events, 0.0 us)
Async XLA Ops:
  0.7 0.7 copy-start.2
  0.7 0.7 copy-start.3
  116.7 2.0 %copy-start = (f32[512,512]{1,0:T(8,128)S(1)}, f32[512,512]{1,0:T(8,128)}, u32[]{:S(2)}) copy-start(f32[512,512]{1,0:T(8,128)} %get-tuple-element.15) | copy-start | bytes 3145732
  118.7 1.4 %copy-start.1 = (bf16[512,512]{1,0:T(8,128)(2,1)S(1)}, bf16[512,512]{1,0:T(8,128)(2,1)}, u32[]{:S(2)}) copy-start(bf16[512,512]{1,0:T(8,128)(2,1)} %get-tuple-element.16) | copy-start | bytes 1572868

commit v3 on v2

v3 whole, which is shorter than its diff:
```python
import functools
import math

import jax
import jax.numpy as jnp
from jax import lax
from jax.experimental import pallas as pl
from jax.experimental.pallas import tpu as pltpu
from jax.sharding import PartitionSpec as P

TILE = 128
SLOTS = 8
REACH = 2
SPAN = 2 * REACH + 1
GROUP = 4
MESH = pl.DeviceIdType.MESH
BF16 = jnp.bfloat16
F32 = jnp.float32
RUN = 8
PLAN = "XZoooooooorrrzrrrrrffxffyffffc"


def place(nb, run):
    b = lax.axis_index("blk")
    r = lax.axis_index("repl")
    flip = 2 * ((b // run) % 2)
    g = (r + flip) % GROUP
    up = (b + 1) % nb
    down = (b + nb - 1) % nb
    r_up = (g + 2 * ((up // run) % 2)) % GROUP
    r_down = (g + 2 * ((down // run) % 2)) % GROUP
    p1 = r + 1 - 2 * (r % 2)
    p2 = (r + 2) % GROUP
    p3 = (p1 + 2) % GROUP
    return b, r, flip, g, up, down, r_up, r_down, p1, p2, p3


def partners(r):
    p1 = r + 1 - 2 * (r % 2)
    return r, p1, (r + 2) % GROUP, (p1 + 2) % GROUP


def remote(src, dst, send, recv, b, r):
    return pltpu.make_async_remote_copy(
        src_ref=src, dst_ref=dst, send_sem=send, recv_sem=recv, device_id=(b, r), device_id_type=MESH
    )


def greet(peers):
    barrier = pltpu.get_barrier_semaphore()
    for peer in peers:
        pl.semaphore_signal(barrier, inc=1, device_id=peer, device_id_type=MESH)
    pl.semaphore_wait(barrier, len(peers))


def ordered(member):
    own, core, chip, both = partners(member)
    return chip, both, core, own


def columns(ref, block):
    return ref.at[:, :, pl.ds(pl.multiple_of(block * TILE, TILE), TILE)]


def sorted_entries(dest):
    rows = lax.broadcasted_iota(jnp.int32, (TILE, TILE), 0)
    lanes = lax.broadcasted_iota(jnp.int32, (TILE, TILE), 1)
    across = jnp.broadcast_to(dest, (TILE, TILE))

    def count(mask, axis, value=1):
        return jnp.sum(jnp.where(mask, value, 0), axis=axis, keepdims=True)

    down = jnp.broadcast_to(count(rows == lanes, 1, across), (TILE, TILE))
    tie = (across == down) & (lanes < rows)
    rank = jnp.broadcast_to(count((across < down) | tie, 1), (TILE, TILE))
    repeat = jnp.broadcast_to(count(tie, 1), (TILE, TILE)) > 0
    hit = rank == lanes
    order = count(hit, 0, rows)
    before = jnp.where(count(hit & repeat, 0) > 0, lanes[0:1, :] - 1, TILE)
    owner = count(hit, 0, rows // SLOTS)
    upto = count(down <= lanes, 0)
    last = jnp.where(count(down == lanes, 0) > 0, upto - 1, TILE)
    return order, before, owner, last


def layer_kernel(
    nb, run, scale,
    feats, weight, vals, table, cot,
    out, grad, wgrad,
    win, vbuf, tbuf, smv, tsm, wv, cv, aggs, aggr, slope, bts, btp, wt, runs,
    far, su, sd, ru2, rd2, ru1, rd1, tot, rt, a0, s0, a1, s1, a2, s2, a3, b3, whole,
    fs, fr, us, ur, ds_, dr, us2, ur2, ds2, dr2, vs, vr, ts, tr, asend, arecv, bsend, brecv,
    vus, vur, vds, vdr, vus2, vur2, vds2, vdr2, gs, gr,
    w0s, w0r, w1s, w1r, w2s, w2r, w3s, w3r, x3s, x3r, x2s, x2r, x1s, x1r, x0s, x0r, loc,
):
    b, r, flip, g, up, down, r_up, r_down, p1, p2, p3 = place(nb, run)
    deep = nb // (2 * run)
    x_hi, y, z = (b // run) % 2, b // (2 * run), b % run
    core = r % 2
    xi = x_hi * 2 + r // 2
    wide = [(xi + i) % GROUP for i in range(1, GROUP)]
    tall = [(y + i) % deep for i in range(1, deep)]
    along = [(z + i) % run for i in range(1, run)]

    def at_x(i):
        return (y * 2 + i // 2) * run + z, (i % 2) * 2 + core

    def at_y(i):
        return (i * 2 + x_hi) * run + z, r

    def at_z(i):
        return (y * 2 + x_hi) * run + i, r

    panel_peers = (p1, p2, p3)
    order = (p2, p3, p1, r)
    greet(
        [(b, p) for p in panel_peers]
        + [(up, r_up), (down, r_down)]
        + [at_x(i) for i in wide]
        + [at_y(i) for i in tall]
        + [at_z(i) for i in along]
    )

    def group_of(member):
        return (member + flip) % GROUP

    sends = []

    def go(copy):
        copy.start()
        sends.append(copy)

    def landed(dst, recv):
        remote(dst, dst, fs.at[0], recv, b, p1).wait_recv()

    rows = vals.shape[0]
    panel_blocks = GROUP * rows
    dead = SPAN * panel_blocks

    def piece(panel, member):
        return win.at[pl.ds(panel * panel_blocks + member * rows, rows)]

    def tiles(member, c):
        return vbuf.at[pl.ds((member * rows + c) * SLOTS, SLOTS)]

    mine = columns(feats, g)
    for slot, p in enumerate((p2, p3, p1)):
        go(remote(columns(feats, group_of(p)), piece(2, r), fs.at[slot], fr.at[r], b, p))
    go(remote(mine, piece(1, r), us.at[0], ur.at[r], up, r_up))
    go(remote(mine, piece(3, r), ds_.at[0], dr.at[r], down, r_down))
    for slot, p in enumerate((p2, p3, p1)):
        go(remote(table, tbuf.at[r], ts.at[slot], tr.at[r], b, p))
    for c in range(rows):
        go(remote(vals.at[c], tiles(r, c), vs.at[0, c], vr.at[r, c], b, p2))
        go(remote(vals.at[c], tiles(r, c), vs.at[1, c], vr.at[r, c], b, p1))
    own = [
        pltpu.make_async_copy(table, tbuf.at[r], loc.at[0]),
        pltpu.make_async_copy(mine, piece(2, r), loc.at[1]),
        pltpu.make_async_copy(weight, wv, loc.at[2]),
        pltpu.make_async_copy(cot, cv, loc.at[3]),
    ] + [pltpu.make_async_copy(vals.at[c], tiles(r, c), loc.at[4 + c]) for c in range(rows)]
    for copy in own:
        copy.start()
    win[dead] = jnp.zeros((TILE, TILE), BF16)
    runs[TILE] = jnp.zeros((TILE, TILE), F32)

    for slot, p in ((1, p1), (2, p2), (3, p3)):
        landed(piece(2, p), fr.at[p])
        go(remote(piece(2, p), piece(1, p), us.at[slot], ur.at[p], up, r_up))
        go(remote(piece(2, p), piece(3, p), ds_.at[slot], dr.at[p], down, r_down))
    for p in panel_peers:
        landed(tbuf.at[p], tr.at[p])
    own[0].wait()
    dest = (tbuf[0] + tbuf[1]) + (tbuf[2] + tbuf[3])
    smv[0] = dest
    for line, value in enumerate(sorted_entries(dest[0:1, :])):
        smv[line + 1] = jnp.broadcast_to(value, (8, TILE))
    to_scalars = pltpu.make_async_copy(smv, tsm, loc.at[0])
    to_scalars.start()

    from_below = partners(r_down)
    from_above = partners(r_up)
    for slot in range(GROUP):
        i = from_below[slot]
        landed(piece(1, i), ur.at[i])
        go(remote(piece(1, i), piece(0, i), us2.at[slot], ur2.at[i], up, r_up))
        i = from_above[slot]
        landed(piece(3, i), dr.at[i])
        go(remote(piece(3, i), piece(4, i), ds2.at[slot], dr2.at[i], down, r_down))
        if slot < rows:
            landed(tiles(p2, slot), vr.at[p2, slot])
            go(remote(tiles(p2, slot), tiles(p2, slot), vs.at[2, slot], vr.at[p2, slot], b, p1))
    for i in range(GROUP):
        landed(piece(0, i), ur2.at[i])
        landed(piece(4, i), dr2.at[i])
    for copy in own[1:]:
        copy.wait()
    to_scalars.wait()
    for p in (p1, p3):
        for c in range(rows):
            landed(tiles(p, c), vr.at[p, c])

    half = rows // 2
    halves = [pl.ds(h * half * TILE, half * TILE) for h in range(2)]
    stay = []
    for h in range(2):
        for slot, q in enumerate(order):

            def one_row(kk, carry, q=q):
                first = (q * rows + kk) * SLOTS
                left = [vbuf[first + s] for s in range(SLOTS)]
                right = [win[tsm[0, 0, first + s]] for s in range(SLOTS)]
                total = jnp.dot(
                    jnp.concatenate(left, axis=1), jnp.concatenate(right, axis=0), preferred_element_type=F32
                )
                aggs[q, pl.ds(pl.multiple_of(kk * TILE, TILE), TILE), :] = total.astype(BF16)
                return carry

            lax.fori_loop(h * half, (h + 1) * half, one_row, 0)
            block, dst = aggs.at[q, halves[h]], aggr.at[g, halves[h]]
            if slot < 3:
                go(remote(block, dst, asend.at[slot, h], arecv.at[g, h], b, q))
            else:
                stay.append(pltpu.make_async_copy(block, dst, loc.at[4 + h]))
                stay[-1].start()

    def dense(t, carry):
        span = pl.ds(pl.multiple_of(t * TILE, TILE), TILE)
        agg = jnp.concatenate([aggr[i, span, :] for i in range(GROUP)], axis=1)
        pre = jnp.dot(agg, wv[...], preferred_element_type=F32)
        sigma = jax.nn.sigmoid(pre)
        out[span, :] = (pre * sigma).astype(BF16)
        slant = cv[span, :].astype(F32) * (sigma * (1.0 + pre * (1.0 - sigma)))
        slope[span, :] = slant.astype(BF16)
        return carry

    for h in range(2):
        stay[h].wait()
        for p in panel_peers:
            gp = group_of(p)
            landed(aggr.at[gp, halves[h]], arecv.at[gp, h])
        lax.fori_loop(h * half, (h + 1) * half, dense, 0)
        for slot, q in enumerate(order):
            part = wv[pl.ds(pl.multiple_of(group_of(q) * TILE, TILE), TILE), :]
            for t in range(h * half, (h + 1) * half):
                turned = lax.dot_general(
                    part, slope[pl.ds(t * TILE, TILE), :], (((1,), (1,)), ((), ())), preferred_element_type=F32
                )
                if slot < 3:
                    bts[slot, t] = turned.astype(BF16)
                else:
                    btp[r * rows + t] = turned.astype(BF16)
            if slot < 3:
                block, dst = bts.at[slot, pl.ds(h * half, half)], btp.at[pl.ds(r * rows + h * half, half)]
                go(remote(block, dst, bsend.at[slot, h], brecv.at[r, h], b, q))

    def weight_rows(i):
        wt[i] = lax.dot_general(aggr[i], slope[...], (((0,), (0,)), ((), ())), preferred_element_type=F32)

    for i in range(2):
        theirs = 2 * (1 - core) + i
        weight_rows(theirs)
        go(remote(wt.at[theirs], a0.at[i], w0s.at[i], w0r.at[i], b, p1))
    quarter = wt.shape[1]
    for i in range(2):
        weight_rows(2 * core + i)
    for i in range(2):
        landed(a0.at[i], w0r.at[i])
        s0[pl.ds(i * quarter, quarter), :] = wt[2 * core + i] + a0[i]
    block = 2 * quarter // deep
    for slot, i in enumerate(tall):
        part = s0.at[pl.ds(pl.multiple_of(i * block, block), block), :]
        go(remote(part, a1.at[y], w1s.at[slot], w1r.at[y], *at_y(i)))
    for p in panel_peers:
        for h in range(2):
            landed(btp.at[pl.ds(p * rows + h * half, half)], brecv.at[p, h])

    def eight(t, carry):
        first = t * 8
        terms = [
            jnp.dot(btp[tsm[3, 0, first + i]], vbuf[tsm[1, 0, first + i]], preferred_element_type=F32)
            for i in range(8)
        ]
        for i in range(8):
            runs[first + i] = terms[i] + runs[tsm[2, 0, first + i]]
        return carry

    lax.fori_loop(0, panel_blocks * SLOTS // 8, eight, 0)

    def share(panel, q, t):
        return runs[tsm[4, 0, panel * panel_blocks + q * rows + t]]

    order_below = ordered(r_down)
    order_above = ordered(r_up)
    steps = 2 * GROUP

    def tiles_of(members, step):
        q, h = members[step // 2], step % 2
        return q, q * 2 + h, range(h * half, (h + 1) * half)

    def outward(step):
        q, i, span = tiles_of(order, step)
        for j, t in enumerate(span):
            far[0, i, j] = share(4, q, t).astype(BF16)
            far[1, i, j] = share(0, q, t).astype(BF16)
        go(remote(far.at[0, i], ru2.at[i], vus.at[step], vur.at[i], up, r_up))
        go(remote(far.at[1, i], rd2.at[i], vds.at[step], vdr.at[i], down, r_down))

    def relay(step):
        q, i, span = tiles_of(order_below, step)
        landed(ru2.at[i], vur.at[i])
        for j, t in enumerate(span):
            su[i, j] = (ru2[i, j].astype(F32) + share(3, q, t)).astype(BF16)
        go(remote(su.at[i], ru1.at[i], vus2.at[step], vur2.at[i], up, r_up))
        q, i, span = tiles_of(order_above, step)
        landed(rd2.at[i], vdr.at[i])
        for j, t in enumerate(span):
            sd[i, j] = (rd2[i, j].astype(F32) + share(1, q, t)).astype(BF16)
        go(remote(sd.at[i], rd1.at[i], vds2.at[step], vdr2.at[i], down, r_down))

    def finish(step):
        q, i, span = tiles_of(order, step)
        h = step % 2
        landed(ru1.at[i], vur2.at[i])
        landed(rd1.at[i], vdr2.at[i])
        for j, t in enumerate(span):
            total = share(2, q, t) + (ru1[i, j].astype(F32) + rd1[i, j].astype(F32))
            if step < steps - 2:
                tot[i, j] = total.astype(BF16)
            else:
                rt[g * 2 + h, j] = total.astype(BF16)
        if step < steps - 2:
            go(remote(tot.at[i], rt.at[g * 2 + h], gs.at[step], gr.at[g * 2 + h], b, q))

    line = block // GROUP
    lanes = min(run, 4)
    high, broad = line // (run // lanes), wt.shape[2] // lanes

    def corner(ref, i):
        return ref.at[
            pl.ds(pl.multiple_of((i // lanes) * high, high), high),
            pl.ds(pl.multiple_of((i % lanes) * broad, broad), broad),
        ]

    def over_x():
        total = s0[pl.ds(pl.multiple_of(y * block, block), block), :]
        for i in tall:
            landed(a1.at[i], w1r.at[i])
            total = total + a1[i]
        s1[...] = total
        for slot, i in enumerate(wide):
            part = s1.at[pl.ds(pl.multiple_of(i * line, line), line), :]
            go(remote(part, a2.at[xi], w2s.at[slot], w2r.at[xi], *at_x(i)))

    def over_z():
        total = s1[pl.ds(pl.multiple_of(xi * line, line), line), :]
        for i in wide:
            landed(a2.at[i], w2r.at[i])
            total = total + a2[i]
        s2[...] = total
        for slot, i in enumerate(along):
            go(remote(corner(s2, i), a3.at[z], w3s.at[slot], w3r.at[z], *at_z(i)))

    def back_z():
        total = corner(s2, z)[...]
        for i in along:
            landed(a3.at[i], w3r.at[i])
            total = total + a3[i]
        corner(b3, z)[...] = total * scale
        for slot, i in enumerate(along):
            go(remote(corner(b3, z), corner(b3, z), x3s.at[slot], x3r.at[z], *at_z(i)))

    def back_x():
        for i in along:
            landed(corner(b3, i), x3r.at[i])
        whole[core, y, xi] = b3[...].astype(BF16)
        mine = whole.at[core, y, xi]
        for slot, i in enumerate(wide):
            go(remote(mine, mine, x2s.at[slot], x2r.at[xi], *at_x(i)))

    def hand_over(i, slot):
        theirs = whole.at[core, i]
        go(remote(theirs, theirs, x0s.at[slot], x0r.at[i], b, p1))

    def back_y():
        for i in wide:
            landed(whole.at[core, y, i], x2r.at[i])
        mine = whole.at[core, y]
        for slot, i in enumerate(tall):
            go(remote(mine, mine, x1s.at[slot], x1r.at[y], *at_y(i)))
        hand_over(y, 0)

    def back_core():
        for slot, i in enumerate(tall):
            landed(whole.at[core, i], x1r.at[i])
            hand_over(i, slot + 1)

    turns = {"o": iter(range(steps)), "r": iter(range(steps)), "f": iter(range(steps))}
    acts = {"o": outward, "r": relay, "f": finish}
    once = {"X": over_x, "Z": over_z, "z": back_z, "x": back_x, "y": back_y, "c": back_core}
    for turn in PLAN:
        if turn in acts:
            acts[turn](next(turns[turn]))
        else:
            once[turn]()

    eye = (
        lax.broadcasted_iota(jnp.int32, (TILE, TILE), 0) == lax.broadcasted_iota(jnp.int32, (TILE, TILE), 1)
    ).astype(BF16)
    for p in panel_peers:
        gp = group_of(p)
        for h in range(2):
            landed(rt.at[gp * 2 + h], gr.at[gp * 2 + h])
    for i in range(GROUP):
        for t in range(rows):
            turned = lax.dot_general(eye, rt[i * 2 + t // half, t % half], (((1,), (1,)), ((), ())), preferred_element_type=F32)
            grad[pl.ds(t * TILE, TILE), pl.ds(i * TILE, TILE)] = turned.astype(BF16)
    for i in range(deep):
        landed(whole.at[1 - core, i], x0r.at[i])
    for c in range(2):
        for i in range(deep):
            for j in range(GROUP):
                wgrad[pl.ds((c * deep + i) * block + j * line, line), :] = whole[c, i, j].astype(F32)
    for copy in sends:
        copy.wait_send()


def window_table(tile_cols, tile_count, panel_blocks, nb):
    center = lax.axis_index("blk")
    offset = (tile_cols // panel_blocks - center) % nb
    offset = jnp.where(offset > REACH, offset - nb, offset)
    index = (offset + REACH) * panel_blocks + tile_cols % panel_blocks
    dead = SPAN * panel_blocks
    alive = jnp.arange(SLOTS, dtype=jnp.int32)[None, :] < tile_count[:, None]
    index = jnp.where(alive, jnp.clip(index, 0, dead - 1), dead).astype(jnp.int32)
    line = jnp.tile(index.reshape(1, -1), (8, GROUP))
    lane = lax.broadcasted_iota(jnp.int32, line.shape, 1)
    return jnp.where(lane // index.size == lax.axis_index("repl"), line, 0)


def local(nb, run, feats, weight, vals, cols, count, cot):
    nodes, width = feats.shape
    rows = nodes // TILE
    panel_blocks = GROUP * rows
    deep = nb // (2 * run)
    table = window_table(cols, count, panel_blocks, nb)
    anywhere = pl.BlockSpec(memory_space=pl.ANY)
    dma = pltpu.SemaphoreType.DMA
    shape = jax.ShapeDtypeStruct
    chunk = (2 * GROUP, rows // 2, TILE, TILE)
    quarter = width // GROUP
    block = 2 * quarter // deep
    line = block // GROUP
    lanes = min(run, 4)
    corner = (line // (run // lanes), width // lanes)
    in_hbm = pl.BlockSpec(memory_space=pltpu.HBM)
    in_vmem = pl.BlockSpec(memory_space=pltpu.VMEM)
    pair = [dma((GROUP,)), dma((GROUP,))]
    out, grad, wgrad = pl.pallas_call(
        functools.partial(layer_kernel, nb, run, 1.0 / math.sqrt(nodes * GROUP * nb)),
        out_shape=(
            shape((nodes, width), BF16),
            shape((nodes, width), BF16),
            shape((width, width), F32),
        ),
        in_specs=[in_hbm, in_hbm, in_hbm, anywhere, in_hbm],
        out_specs=(in_vmem,) * 3,
        scratch_shapes=[
            pltpu.VMEM((SPAN * panel_blocks + 1, TILE, TILE), BF16),
            pltpu.VMEM((panel_blocks * SLOTS, TILE, TILE), BF16),
            pltpu.VMEM((GROUP, 8, TILE), jnp.int32),
            pltpu.VMEM((5, 8, TILE), jnp.int32),
            pltpu.SMEM((5, 8, TILE), jnp.int32),
            pltpu.VMEM((width, width), BF16),
            pltpu.VMEM((nodes, width), BF16),
            pltpu.VMEM((GROUP, nodes, TILE), BF16),
            pltpu.VMEM((GROUP, nodes, TILE), BF16),
            pltpu.VMEM((nodes, width), BF16),
            pltpu.VMEM((GROUP - 1, rows, TILE, TILE), BF16),
            pltpu.VMEM((panel_blocks, TILE, TILE), BF16),
            pltpu.VMEM((GROUP, quarter, width), F32),
            pltpu.VMEM((panel_blocks * SLOTS + 1, TILE, TILE), F32),
            pltpu.VMEM((2,) + chunk, BF16),
        ]
        + [pltpu.VMEM(chunk, BF16)] * 8
        + [
            pltpu.VMEM((2, quarter, width), F32),
            pltpu.VMEM((2 * quarter, width), F32),
            pltpu.VMEM((deep, block, width), F32),
            pltpu.VMEM((block, width), F32),
            pltpu.VMEM((GROUP, line, width), F32),
            pltpu.VMEM((line, width), F32),
            pltpu.VMEM((run,) + corner, F32),
            pltpu.VMEM((line, width), F32),
            pltpu.VMEM((2, deep, GROUP, line, width), BF16),
        ]
        + pair * 5
        + [dma((3, rows)), dma((GROUP, rows))]
        + pair
        + [dma((3, 2)), dma((GROUP, 2))] * 2
        + [dma((2 * GROUP,)), dma((2 * GROUP,))] * 5
        + [dma((2,)), dma((2,))]
        + [dma((deep,)), dma((deep,))]
        + pair
        + [dma((run,)), dma((run,))] * 2
        + pair
        + [dma((deep,)), dma((deep,))] * 2
        + [dma((8,))],
        compiler_params=pltpu.CompilerParams(
            collective_id=0, has_side_effects=True, vmem_limit_bytes=50 << 20
        ),
        name="layer",
    )(feats.reshape(rows, TILE, width), weight, vals, table, cot)
    return out, wgrad, grad


def solution(mesh, run=RUN):
    both = ("blk", "repl")
    in_specs = (
        P(both, None),
        P(),
        P(both, None, None, None),
        P(both, None),
        P(both),
        P(both, None),
    )
    out_specs = (P(both, None), P(), P(both, None))
    body = functools.partial(local, mesh.shape["blk"], run)
    return jax.shard_map(body, mesh=mesh, in_specs=in_specs, out_specs=out_specs, check_vma=False)
```

time: 121 us -> 112 us (0.926)
  Pallas kernels: 114 us -> 104 us
  local copies, waits for them, and re-layouts: 5 us -> 6.53 us
    pallas_call x1, Pallas kernels: 114 us -> 104 us  [local(): pl.pallas_call(functools.partial(layer_kernel, nb, run, 1.0 / math.sqrt(n...]
    unnamed x11 -> x13, local copies, waits for them, and re-layouts: 4.82 us -> 6.35 us
where the time goes in v3:
time: 112 us; the launch traced here: 111 us
  Pallas kernels  104 us (93%)
  local copies, waits for them, and re-layouts  6.53 us (6%)
    pallas_call x1, Pallas kernels, local(): pl.pallas_call(functools.partial(layer_kernel, nb, run, 1.0 / math.sqrt(n...  104 us
    unnamed x13, local copies, waits for them, and re-layouts  6.35 us

profile of v3, /device:TPU:1, one launch (start us, length us, event | category | flops | bytes accessed | tf_op | source)
XLA Modules:
  0.0 111.4 jit_solution(4463905153097920015)
XLA Ops:
  0.7 0.0 copy-start.3
  0.7 0.0 copy-start.4
  0.7 0.7 copy-done.3
  1.3 0.0 copy-done.4
  1.3 0.1 fusion.5
  1.4 0.1 tile.12
  1.5 0.1 tile.14
  1.6 0.0 copy-start
  1.6 1.0 copy-done
  2.6 0.0 copy-start.1
  2.7 1.0 copy-done.1
  3.7 0.0 copy-start.2
  3.7 1.0 copy-done.2
  4.7 104.1 %layer.1 = (bf16[512,512]{1,0:T(8,128)(2,1)S(1)}, bf16[512,512]{1,0:T(8,128)(2,1)S(1)}, f32[512,512]{1,0:T(8,128)S(1)}) custom-call(bf16[4,128,512]{2,1,0:T(8,128)(2,1)S(1)} %bitcast.1, bf16[512,512]{1,0:T(8,128)(2,1)S(1)} %copy-done.1, bf16[4,8,128,128]{3,2,1,0:T(8,128)(2,1)} %vals.1, s32[8,128]{1,0:T(8,128)S(1)} %fusion.table, bf16[512,512]{1,0:T(8,128)(2,1)S(1)} %copy-done.2), custom_call_target="tpu_custom_call" | custom-call | tf_op jit(solution)/shard_map/layer/pallas_call | solution.py:459
  108.8 0.8 copy.12
  109.6 1.0 copy.13
  110.6 0.8 copy.14
  (4 shorter events, 0.0 us)
Async XLA Ops:
  0.7 0.7 copy-start.3
  0.7 0.7 copy-start.4
  1.6 1.0 copy-start
  2.6 1.0 copy-start.1
  3.7 1.0 copy-start.2

commit v4 on v3

--- a/solution.py
+++ b/solution.py
@@ -17,7 +17,7 @@
 BF16 = jnp.bfloat16
 F32 = jnp.float32
 RUN = 8
-PLAN = "XZoooooooorrrzrrrrrffxffyffffc"
+PLAN = "XZoooooooorrrzrrrrrxyffcffffff"
 
 
 def place(nb, run):
@@ -187,23 +187,30 @@
         i = from_above[slot]
         landed(piece(3, i), dr.at[i])
         go(remote(piece(3, i), piece(4, i), ds2.at[slot], dr2.at[i], down, r_down))
-        if slot < rows:
-            landed(tiles(p2, slot), vr.at[p2, slot])
-            go(remote(tiles(p2, slot), tiles(p2, slot), vs.at[2, slot], vr.at[p2, slot], b, p1))
+
+    def tiles_on(c):
+        landed(tiles(p2, c), vr.at[p2, c])
+        go(remote(tiles(p2, c), tiles(p2, c), vs.at[2, c], vr.at[p2, c], b, p1))
+
+    half = rows // 2
+    for c in range(half):
+        tiles_on(c)
     for i in range(GROUP):
         landed(piece(0, i), ur2.at[i])
         landed(piece(4, i), dr2.at[i])
     for copy in own[1:]:
         copy.wait()
     to_scalars.wait()
-    for p in (p1, p3):
-        for c in range(rows):
-            landed(tiles(p, c), vr.at[p, c])
-
-    half = rows // 2
+
     halves = [pl.ds(h * half * TILE, half * TILE) for h in range(2)]
     stay = []
     for h in range(2):
+        for c in range(h * half, (h + 1) * half):
+            if h == 1:
+                tiles_on(c)
+            landed(tiles(p1, c), vr.at[p1, c])
+        for c in range(h * half, (h + 1) * half):
+            landed(tiles(p3, c), vr.at[p3, c])
         for slot, q in enumerate(order):
 
             def one_row(kk, carry, q=q):
@@ -510,7 +517,11 @@
             collective_id=0, has_side_effects=True, vmem_limit_bytes=50 << 20
         ),
         name="layer",
-    )(feats.reshape(rows, TILE, width), weight, vals, table, cot)
+    )(
+        *(pltpu.with_memory_space_constraint(x, pltpu.HBM) for x in (feats.reshape(rows, TILE, width), weight, vals)),
+        table,
+        pltpu.with_memory_space_constraint(cot, pltpu.HBM),
+    )
     return out, wgrad, grad
 
 

time: 112 us -> 106 us (0.946)
  local copies, waits for them, and re-layouts: 6.53 us -> 3.4 us
  Pallas kernels: 104 us -> 101 us
    unnamed x13 -> x7, local copies, waits for them, and re-layouts: 6.35 us -> 3.23 us
    pallas_call x1, Pallas kernels: 104 us -> 101 us  [local(): pl.pallas_call(functools.partial(layer_kernel, nb, run, 1.0 / math.sqrt(n...]
where the time goes in v4:
time: 106 us
  Pallas kernels  101 us (95%)
  local copies, waits for them, and re-layouts  3.4 us (3%)
    pallas_call x1, Pallas kernels, local(): pl.pallas_call(functools.partial(layer_kernel, nb, run, 1.0 / math.sqrt(n...  101 us
    unnamed x7, local copies, waits for them, and re-layouts  3.23 us

profile of v4, /device:TPU:1, one launch (start us, length us, event | category | flops | bytes accessed | tf_op | source)
XLA Modules:
  0.0 105.6 jit_solution(16326156616335159687)
XLA Ops:
  0.7 0.0 copy-start
  0.7 0.0 copy-start.1
  0.7 0.7 copy-done
  1.3 0.0 copy-done.1
  1.3 0.1 fusion.5
  1.4 0.1 tile.12
  1.5 0.1 tile.14
  1.6 101.4 %layer.1 = (bf16[512,512]{1,0:T(8,128)(2,1)S(1)}, bf16[512,512]{1,0:T(8,128)(2,1)S(1)}, f32[512,512]{1,0:T(8,128)S(1)}) custom-call(bf16[4,128,512]{2,1,0:T(8,128)(2,1)} %bitcast.1, bf16[512,512]{1,0:T(8,128)(2,1)} %weight.1, bf16[4,8,128,128]{3,2,1,0:T(8,128)(2,1)} %vals.1, s32[8,128]{1,0:T(8,128)S(1)} %fusion.table, bf16[512,512]{1,0:T(8,128)(2,1)} %cot.1), custom_call_target="tpu_custom_call" | custom-call | tf_op jit(solution)/shard_map/layer/pallas_call | solution.py:466
  103.0 0.8 copy.12
  103.8 1.0 copy.13
  104.8 0.8 copy.14
  (4 shorter events, 0.0 us)
Async XLA Ops:
  0.7 0.7 copy-start
  0.7 0.7 copy-start.1

commit v5 on v4

--- a/solution.py
+++ b/solution.py
@@ -17,7 +17,7 @@
 BF16 = jnp.bfloat16
 F32 = jnp.float32
 RUN = 8
-PLAN = "XZoooooooorrrzrrrrrxyffcffffff"
+PLAN = "ooooooooXrZrrrrzrrrxfyfcffffff"
 
 
 def place(nb, run):

time: 106 us -> 105 us (level)
  no operation moved by 1% of the time
where the time goes in v5:
time: 105 us
  Pallas kernels  101 us (96%)
  local copies, waits for them, and re-layouts  3.4 us (3%)
    pallas_call x1, Pallas kernels, local(): pl.pallas_call(functools.partial(layer_kernel, nb, run, 1.0 / math.sqrt(n...  101 us
    unnamed x7, local copies, waits for them, and re-layouts  3.23 us

profile of v5, /device:TPU:1, one launch (start us, length us, event | category | flops | bytes accessed | tf_op | source)
XLA Modules:
  0.0 105.1 jit_solution(14810411621128239549)
XLA Ops:
  0.7 0.0 copy-start
  0.7 0.0 copy-start.1
  0.7 0.7 copy-done
  1.3 0.0 copy-done.1
  1.3 0.1 fusion.5
  1.4 0.1 tile.12
  1.5 0.1 tile.14
  1.6 100.9 %layer.1 = (bf16[512,512]{1,0:T(8,128)(2,1)S(1)}, bf16[512,512]{1,0:T(8,128)(2,1)S(1)}, f32[512,512]{1,0:T(8,128)S(1)}) custom-call(bf16[4,128,512]{2,1,0:T(8,128)(2,1)} %bitcast.1, bf16[512,512]{1,0:T(8,128)(2,1)} %weight.1, bf16[4,8,128,128]{3,2,1,0:T(8,128)(2,1)} %vals.1, s32[8,128]{1,0:T(8,128)S(1)} %fusion.table, bf16[512,512]{1,0:T(8,128)(2,1)} %cot.1), custom_call_target="tpu_custom_call" | custom-call | tf_op jit(solution)/shard_map/layer/pallas_call | solution.py:466
  102.5 0.8 copy.12
  103.3 1.0 copy.13
  104.3 0.8 copy.14
  (4 shorter events, 0.0 us)
Async XLA Ops:
  0.7 0.7 copy-start
  0.7 0.7 copy-start.1
